TPU v7x, 32 devices: a whole 2x2x4 slice. The times are simulated.
32 devices in a mesh: row: 4 (over y, x), col: 8 (over z, core).
Axes of the slice: x: 2, y: 2, z: 4, core: 2. Of those that a mesh axis runs over, the one named last changes fastest.
Arguments:
- amps_old: bfloat16 [1024, 262144], P(('row', 'col')), may hold values from -6 to 6
- other_terms: bfloat16 [1024, 262144], P(('row', 'col')), may hold values from -6 to 6
- occ_energy: float32 [32], replicated, may hold values from -1.5 to -0.5
- virt_energy: float32 [512], replicated, may hold values from 0.2 to 1.5
- integrals: bfloat16 [1024, 262144], P('row', 'col'), may hold values from -0.1875 to 0.1875
Outputs:
- amps_new: bfloat16 [1024, 262144], P(('row', 'col'))
All inputs are finite; a program needn't handle non-finite values.
Results may differ from a plain program's by a relative error of at most 0.0055.
Values may be sent and summed in bfloat16 or wider, within the bound.
No kernel may reach another device: no remote copies, remote signals or barrier semaphores. Data moves between devices by JAX's collectives and lax.ppermute only.
A program may use at most 320 MiB of HBM per device.

v0:
```python
import jax
import jax.numpy as jnp
from jax import lax
from jax.sharding import PartitionSpec as P


def pair_energy(pairs, occ_energy):
    count = occ_energy.shape[0]
    first = pairs // count
    second = pairs % count
    grid = jnp.arange(count, dtype=jnp.int32)
    e_first = jnp.sum(jnp.where(first[:, None] == grid[None, :], occ_energy[None, :], 0.0), axis=1)
    e_second = jnp.sum(
        jnp.where(second[:, None] == grid[None, :], occ_energy[None, :], 0.0), axis=1
    )
    return e_first + e_second


def local(amps_old, other_terms, occ_energy, virt_energy, integrals):
    n_row = lax.axis_size("row")
    n_col = lax.axis_size("col")
    row_id = lax.axis_index("row")
    col_id = lax.axis_index("col")
    per_dev = amps_old.shape[0]
    cd_dev = integrals.shape[0]
    window = amps_old[:, : cd_dev * n_row]
    row_pairs = lax.all_gather(window, "col", axis=0, tiled=True)
    panel = lax.all_to_all(row_pairs, "row", split_axis=1, concat_axis=0, tiled=True)
    ladder = lax.psum_scatter(
        jnp.dot(panel, integrals, preferred_element_type=jnp.float32).astype(jnp.bfloat16),
        "row",
        scatter_dimension=0,
        tiled=True,
    ).astype(jnp.float32)
    virt_all = (virt_energy[:, None] + virt_energy[None, :]).reshape(-1)
    first_pair = (row_id * n_col + col_id) * per_dev
    own_pairs = first_pair + jnp.arange(per_dev, dtype=jnp.int32)
    denom_pairs = pair_energy(own_pairs, occ_energy)[:, None] - virt_all[None, :]
    moved = lax.all_to_all(
        ladder.astype(jnp.bfloat16), "col", split_axis=0, concat_axis=1, tiled=True
    ).astype(ladder.dtype)
    increment = (moved / denom_pairs).astype(jnp.bfloat16)
    updated = (
        amps_old.astype(jnp.float32)
        + other_terms.astype(jnp.float32) / denom_pairs
        + increment.astype(jnp.float32)
    )
    return updated.astype(jnp.bfloat16)


def solution(mesh):
    return jax.shard_map(
        local,
        mesh=mesh,
        in_specs=(P(("row", "col"), None), P(("row", "col"), None), P(), P(), P("row", "col")),
        out_specs=P(("row", "col"), None),
        check_vma=False,
    )
```

profile of v0, /device:TPU:0, one launch (start us, length us, event | category | flops | bytes accessed | tf_op | source)
XLA Modules:
  0.0 1049.0 jit_solution(17985617899202413814)
XLA Ops:
  6.5 0.0 reduce-scatter.4.cloned.1.call-start
  6.5 0.8 slice.3
  7.4 16.5 %all_gather.3 = bf16[256,1024]{1,0:T(8,128)(2,1)S(1)} all-gather(bf16[32,1024]{1,0:T(8,128)(2,1)S(1)} %slice.3), channel_id=1, replica_groups=mesh['row'=4,'col'=8] {'col'}, dimensions={0}, use_global_device_ids=true | all-gather | bytes 589824 | tf_op jit(solution)/shard_map/all_gather | solution.py:27
  23.9 0.2 copy.14
  24.1 12.5 %all_to_all.32 = bf16[256,4,256]{0,2,1:T(8,128)(2,1)S(1)} all-to-all(bf16[256,4,256]{0,2,1:T(8,128)(2,1)S(1)} %bitcast.18), channel_id=1, replica_groups=mesh['row'=4,'col'=8] {'row'}, dimensions={1} | all-to-all | bytes 1048576 | tf_op jit(solution)/shard_map/all_to_all | solution.py:28
  36.6 0.2 copy.15
  36.8 30.6 %convolution_convert_fusion = bf16[1024,32768]{1,0:T(8,128)(2,1)} fusion(bf16[1024,256]{1,0:T(8,128)(2,1)S(1)} %bitcast.16, bf16[256,32768]{1,0:T(8,128)(2,1)} %param.9), kind=kOutput, calls=%fused_computation | convolution fusion | flops 17213423616 | bytes 84410368 | tf_op jit(solution)/shard_map/dot_general | solution.py:30
  67.4 0.0 reduce-scatter.4.cloned.1.call-update
  67.4 0.0 copy-start
  67.4 0.0 copy-start.1
  67.5 557.9 %reduce-scatter.4.cloned.1.call-done = bf16[256,32768]{1,0:T(8,128)(2,1)} async-done(((bf16[1024,32768]{1,0:T(8,128)(2,1)}), bf16[256,32768]{1,0:T(8,128)(2,1)}) %reduce-scatter.4.cloned.1.call-update) | async-done | bytes 16777232
  625.4 5.8 all-to-all-start.1
  631.1 0.0 copy-done
  631.1 0.1 add_bitcast_fusion
  631.3 0.3 copy.18
  631.6 0.0 copy-done.1
  631.6 0.2 select_reduce_fusion
  631.8 363.0 %all-to-all-done.1 = bf16[8,32,32768]{2,1,0:T(8,128)(2,1)} async-done(((bf16[8,32,32768]{2,1,0:T(8,128)(2,1)}), bf16[8,32,32768]{2,1,0:T(8,128)(2,1)}, u32[]{:S(2)}, u32[]{:S(2)}) %all-to-all-start.1) | async-done | bytes 16777248 | tf_op jit(solution)/shard_map/all_to_all | solution.py:39
  994.8 8.5 convert_bitcast_fusion
  1003.3 11.2 %copy.17 = f32[8,4,8,32768]{3,2,0,1:T(8,128)} copy(f32[8,4,8,32768]{3,2,1,0:T(8,128)S(1)} %convert_bitcast_fusion) | data formatting | bytes 67108864 | tf_op jit(solution)/shard_map/convert_element_type | solution.py:41
  1014.5 27.6 %fusion.3 = bf16[32,262144]{1,0:T(8,128)(2,1)} fusion(bf16[32,262144]{1,0:T(8,128)(2,1)} %param.6, bf16[32,262144]{1,0:T(8,128)(2,1)} %param.5, f32[32,262144]{1,0:T(8,128)} %bitcast.14, f32[262144]{0:T(1024)S(1)} %bitcast.17, f32[32]{0:T(128)S(1)} %add.70), kind=kLoop, calls=%fused_computation.7 | loop fusion | flops 83886080 | bytes 84934784 | tf_op jit(solution)/shard_map/convert_element_type | solution.py:48
  (2 shorter events, 0.0 us)
Async XLA Ops:
  6.5 618.8 %reduce-scatter.4.cloned.1.call-start = ((), (), s32[]{:S(2)}) async-start(), calls=%async_computation.3 | async-start | bytes 83886080
  67.4 563.7 %copy-start = (f32[512]{0:T(512)S(1)}, f32[512]{0:T(512)}, u32[]{:S(2)}) copy-start(f32[512]{0:T(512)} %param.8) | copy-start | bytes 6148
  67.4 564.1 %copy-start.1 = (f32[32]{0:T(128)S(1)}, f32[32]{0:T(128)}, u32[]{:S(2)}) copy-start(f32[32]{0:T(128)} %param.7) | copy-start | bytes 388
  625.4 369.4 %all-to-all-start.1 = ((bf16[8,32,32768]{2,1,0:T(8,128)(2,1)}), bf16[8,32,32768]{2,1,0:T(8,128)(2,1)}, u32[]{:S(2)}, u32[]{:S(2)}) async-start(bf16[8,32,32768]{2,1,0:T(8,128)(2,1)} %bitcast.15), calls=%async_computation.1 | async-start | bytes 33554432 | tf_op jit(solution)/shard_map/all_to_all | solution.py:39
Sparse Core Ops, SparseCore 0:
  67.6 557.7 reduce-scatter.3
where the time goes:
time: 1050 us
  waiting for transfers between devices  921 us (88%)
  other arithmetic  36.5 us (3%)
  matrix products  30.6 us (3%)
  blocking collectives  29 us (3%)
  between operations  13.5 us (1%)
  local copies, waits for them, and re-layouts  12.7 us (1%)
    unnamed x2, waiting for transfers between devices  558 us
    all_to_all x1, waiting for transfers between devices, local(): lax.all_to_all(ladder.astype(jnp.bfloat16), 'col', split_axis=0, concat_a...  363 us
    dot_general x1, matrix products, local(): jnp.dot(panel, integrals, preferred_element_type=jnp.float32)  30.6 us
    convert_element_type x1, other arithmetic, local(): return updated.astype(jnp.bfloat16)  27.6 us
  transfers between devices with their start and end apart: 2, of which 2 were waited for; matrix products, arithmetic and copies ran while one was open for 0% of the time, Pallas kernels for 0%

commit v1 on v0

v1 whole, which is shorter than its diff:
```python
import functools

import jax
import jax.numpy as jnp
from jax import lax
from jax.experimental import pallas as pl
from jax.experimental.pallas import tpu as pltpu
from jax.sharding import PartitionSpec as P

CHUNKS = 16


def pair_energy(pairs, occ_energy):
    count = occ_energy.shape[0]
    first = pairs // count
    second = pairs % count
    grid = jnp.arange(count, dtype=jnp.int32)
    e_first = jnp.sum(jnp.where(first[:, None] == grid[None, :], occ_energy[None, :], 0.0), axis=1)
    e_second = jnp.sum(
        jnp.where(second[:, None] == grid[None, :], occ_energy[None, :], 0.0), axis=1
    )
    return e_first + e_second


def contract_body(n_extra, t_ref, own_ref, far_ref, *refs):
    depth = own_ref.shape[0]
    outs = refs[n_extra:]
    acc = jnp.dot(t_ref[0, :, :depth], own_ref[...], preferred_element_type=jnp.float32)
    acc += jnp.dot(t_ref[0, :, depth:], far_ref[...], preferred_element_type=jnp.float32)
    for ref in refs[:n_extra]:
        acc += ref[...].astype(jnp.float32)
    rows = outs[0].shape[0]
    for m, out_ref in enumerate(outs):
        out_ref[...] = acc[m * rows : (m + 1) * rows].astype(out_ref.dtype)


def contract(panel, which, own, far, start, tile, extra=(), pieces=1):
    _, rows, depth2 = panel.shape
    depth, width = far.shape
    base = start // tile
    n_extra = len(extra)
    share = rows // pieces
    return pl.pallas_call(
        functools.partial(contract_body, n_extra),
        grid=(width // tile,),
        in_specs=[
            pl.BlockSpec((1, rows, depth2), lambda i: (which, 0, 0)),
            pl.BlockSpec((depth, tile), lambda i: (0, base + i)),
            pl.BlockSpec((depth, tile), lambda i: (0, i)),
        ]
        + [pl.BlockSpec((rows, tile), lambda i: (0, i))] * n_extra,
        out_specs=[pl.BlockSpec((share, tile), lambda i: (0, i))] * pieces,
        out_shape=[jax.ShapeDtypeStruct((share, width), jnp.bfloat16)] * pieces,
        cost_estimate=pl.CostEstimate(
            flops=2 * rows * depth2 * width,
            bytes_accessed=2 * width * (depth2 + rows * (1 + n_extra)),
            transcendentals=0,
        ),
    )(panel, own, far, *extra)


def update_body(start, cols, source_ref, va_ref, e_ref, vb_ref, old, other, *refs):
    out, old_buf, other_buf, moved_buf, new_buf, in_sem, out_sem = refs[-7:]
    n_col, rows, width = moved_buf.shape
    moved = refs[:n_col]
    virt = vb_ref.shape[1]

    def place(m):
        return pl.ds(pl.multiple_of(source_ref[m] * cols + start, 128), width)

    def fetches(m):
        return (
            pltpu.make_async_copy(old.at[:, place(m)], old_buf.at[m], in_sem.at[1, m]),
            pltpu.make_async_copy(other.at[:, place(m)], other_buf.at[m], in_sem.at[2, m]),
        )

    def store(m):
        return pltpu.make_async_copy(new_buf.at[m], out.at[:, place(m)], out_sem.at[m])

    for m in range(n_col):
        for copy in fetches(m):
            copy.start()
        pltpu.make_async_copy(moved[m], moved_buf.at[m], in_sem.at[0, m]).start()
    energy = jnp.broadcast_to(e_ref[...], (rows, virt))

    @pl.loop(0, n_col)
    def _(m):
        for copy in fetches(m):
            copy.wait()
        pltpu.make_async_copy(moved[0], moved_buf.at[m], in_sem.at[0, m]).wait()
        first = (source_ref[m] * cols + start) // virt
        for s in range(width // virt):
            part = pl.ds(s * virt, virt)
            inverse = 1.0 / (energy - (va_ref[first + s] + vb_ref[...]))
            top = other_buf[m, :, part].astype(jnp.float32) + moved_buf[m, :, part].astype(jnp.float32)
            new_buf[m, :, part] = (old_buf[m, :, part].astype(jnp.float32) + top * inverse).astype(new_buf.dtype)
        store(m).start()

    for m in range(n_col):
        store(m).wait()


def update(old, other, moved, source, energy, virt_energy, start, out):
    rows, total = old.shape
    n_col = len(moved)
    width = moved[0].shape[1]
    ins = [source, virt_energy, energy, virt_energy[None, :], old, other, *moved]
    specs = [
        pl.BlockSpec(memory_space=pltpu.SMEM),
        pl.BlockSpec(memory_space=pltpu.SMEM),
        pl.BlockSpec(memory_space=pltpu.VMEM),
        pl.BlockSpec(memory_space=pltpu.VMEM),
    ] + [pl.BlockSpec(memory_space=pl.ANY)] * (2 + n_col)
    alias = {}
    if out is not None:
        alias = {len(ins): 0}
        ins.append(out)
        specs.append(pl.BlockSpec(memory_space=pl.ANY))
    return pl.pallas_call(
        functools.partial(update_body, start, total // n_col),
        in_specs=specs,
        out_specs=pl.BlockSpec(memory_space=pl.ANY),
        out_shape=jax.ShapeDtypeStruct((rows, total), old.dtype),
        scratch_shapes=[pltpu.VMEM((n_col, rows, width), jnp.bfloat16)] * 4
        + [pltpu.SemaphoreType.DMA((3, n_col)), pltpu.SemaphoreType.DMA((n_col,))],
        input_output_aliases=alias,
        cost_estimate=pl.CostEstimate(
            flops=8 * n_col * rows * width, bytes_accessed=8 * n_col * rows * width, transcendentals=0
        ),
    )(*ins)


def local(amps_old, other_terms, occ_energy, virt_energy, integrals):
    n_row = lax.axis_size("row")
    n_col = lax.axis_size("col")
    row_id = lax.axis_index("row")
    col_id = lax.axis_index("col")
    per_dev = amps_old.shape[0]
    depth, cols = integrals.shape
    n_hi = n_row // 2
    hi, lo = row_id // 2, row_id % 2
    swap = [(r, r ^ 1) for r in range(n_row)]
    width = cols // CHUNKS

    def shift(value, d):
        perm = [(r, ((r // 2 + d) % n_hi) * 2 + r % 2) for r in range(n_row)]
        return lax.ppermute(value, "row", perm)

    far = []
    whole = integrals
    for k in range(CHUNKS):
        piece = whole[:, k * width : (k + 1) * width]
        whole, piece = lax.optimization_barrier((whole, piece))
        far.append(lax.ppermute(piece, "row", swap))

    window = amps_old[:, : depth * n_row]

    def pick(g):
        return lax.dynamic_slice_in_dim(window, g * 2 * depth, 2 * depth, 1)

    mine = [pick(hi)] + [shift(pick((hi - d) % n_hi), -d) for d in range(1, n_hi)]
    panel = lax.all_gather(jnp.stack(mine), "col", axis=1, tiled=True)
    flipped = jnp.concatenate([panel[..., depth:], panel[..., :depth]], axis=-1)
    panel = jnp.where(lo == 0, panel, flipped)
    source = col_id ^ jnp.arange(n_col, dtype=jnp.int32)
    blocks = panel.reshape(n_hi, n_col, per_dev, 2 * depth)
    panel = jnp.concatenate(
        [lax.dynamic_slice_in_dim(blocks, source[m], 1, 1) for m in range(n_col)], axis=1
    ).reshape(panel.shape)

    first_pair = (row_id * n_col + col_id) * per_dev
    energy = pair_energy(first_pair + jnp.arange(per_dev, dtype=jnp.int32), occ_energy)[:, None]

    out = None
    for k in range(CHUNKS):
        start = k * width
        tile = min(1024, width)
        parts = [contract(panel, d, integrals, far[k], start, tile)[0] for d in range(1, n_hi)]
        got = [shift(part, d) for d, part in enumerate(parts, 1)]
        ladder = contract(panel, 0, integrals, far[k], start, tile, got, n_col)
        moved = [ladder[0]]
        for m in range(1, n_col):
            moved.append(lax.ppermute(ladder[m], "col", [(c, c ^ m) for c in range(n_col)]))
        out = update(amps_old, other_terms, moved, source, energy, virt_energy, start, out)
    return out


def solution(mesh):
    return jax.shard_map(
        local,
        mesh=mesh,
        in_specs=(P(("row", "col"), None), P(("row", "col"), None), P(), P(), P("row", "col")),
        out_specs=P(("row", "col"), None),
        check_vma=False,
    )
```

time: 1050 us -> 1040 us (level)
  waiting for transfers between devices: 921 us -> 597 us
  starting transfers between devices: 5.75 us -> 212 us
  Pallas kernels: 0 us -> 160 us
  other arithmetic: 36.5 us -> 0.33 us
  matrix products: 30.6 us -> 0 us
  local copies, waits for them, and re-layouts: 12.7 us -> 39.7 us
  blocking collectives: 29 us -> 15.2 us
    ppermute x0 -> x145, waiting for transfers between devices: none -> 597 us  [the longest x16 243 us: local(): far.append(lax.ppermute(piece, 'row', swap))]
    unnamed x2 -> x0, waiting for transfers between devices: 558 us -> none
    all_to_all x1 -> x0, waiting for transfers between devices: 363 us -> none  [local(): lax.all_to_all(ladder.astype(jnp.bfloat16), 'col', split_axis=0, concat_a...]
    ppermute x0 -> x145, starting transfers between devices: none -> 212 us  [the longest x112 157 us: local(): lax.ppermute(ladder[m], 'col', [(c, c ^ m) for c in range(n_col)])]
    pallas_call x0 -> x48, Pallas kernels: none -> 160 us  [the longest x32 101 us: contract(): pl.pallas_call(functools.partial(contract_body, n_extra), grid=(width //...]
    slice x1 -> x19, local copies, waits for them, and re-layouts: 0.84 us -> 37.8 us  [the longest x16 36.2 us: local(): piece = whole[:, k * width:(k + 1) * width]]
    dot_general x1 -> x0, matrix products: 30.6 us -> none  [local(): jnp.dot(panel, integrals, preferred_element_type=jnp.float32)]
    convert_element_type x1 -> x0, other arithmetic: 27.6 us -> none  [local(): return updated.astype(jnp.bfloat16)]
  transfers between devices with their start and end apart: 2 -> 145, of which waited for: 2 -> 55; matrix products, arithmetic and copies ran while one was open for 0% -> 4% of each run, Pallas kernels for 0% -> 15%
where the time goes in v1:
time: 1040 us
  waiting for transfers between devices  597 us (57%)
  starting transfers between devices  212 us (20%)
  Pallas kernels  160 us (15%)
  local copies, waits for them, and re-layouts  39.7 us (4%)
  between operations  16.9 us (2%)
  blocking collectives  15.2 us (1%)
    ppermute x16, waiting for transfers between devices, local(): far.append(lax.ppermute(piece, 'row', swap))  243 us
    ppermute x17, waiting for transfers between devices, shift(): return lax.ppermute(value, 'row', perm)  213 us
    ppermute x112, starting transfers between devices, local(): lax.ppermute(ladder[m], 'col', [(c, c ^ m) for c in range(n_col)])  157 us
    ppermute x112, waiting for transfers between devices, local(): lax.ppermute(ladder[m], 'col', [(c, c ^ m) for c in range(n_col)])  141 us
    pallas_call x32, Pallas kernels, contract(): pl.pallas_call(functools.partial(contract_body, n_extra), grid=(width //...  101 us
    pallas_call x16, Pallas kernels, update(): pl.pallas_call(functools.partial(update_body, start, total // n_col), in_...  59 us
    slice x16, local copies, waits for them, and re-layouts, local(): piece = whole[:, k * width:(k + 1) * width]  36.2 us
    ppermute x17, starting transfers between devices, shift(): return lax.ppermute(value, 'row', perm)  28.5 us
  transfers between devices with their start and end apart: 145, of which 55 were waited for; matrix products, arithmetic and copies ran while one was open for 4% of the time, Pallas kernels for 15%

profile of v1, /device:TPU:0, one launch (start us, length us, event | category | flops | bytes accessed | tf_op | source)
XLA Modules:
  0.0 1041.1 jit_solution(8210578902274454598)
XLA Ops:
  30.4 20.6 %collective-permute-done.127.far_ref = bf16[256,2048]{1,0:T(8,128)(2,1)} collective-permute-done((bf16[256,2048]{1,0:T(8,128)(2,1)}, bf16[256,2048]{1,0:T(8,128)(2,1)}, u32[]{:S(2)}, u32[]{:S(2)}) %collective-permute-start.127) | collective-permute-done | bytes 1048608 | tf_op jit(solution)/shard_map/ppermute | solution.py:154
  90.1 15.2 %all_gather.3 = bf16[2,256,512]{2,1,0:T(8,128)(2,1)S(1)} all-gather(bf16[2,32,512]{2,1,0:T(8,128)(2,1)S(1)} %pad_maximum_fusion), channel_id=1, replica_groups=mesh['row'=4,'col'=8] {'col'}, dimensions={1}, use_global_device_ids=true | all-gather | bytes 589824 | tf_op jit(solution)/shard_map/all_gather | solution.py:162
  107.3 11.0 %collective-permute-done.100.far_ref = bf16[256,2048]{1,0:T(8,128)(2,1)} collective-permute-done((bf16[256,2048]{1,0:T(8,128)(2,1)}, bf16[256,2048]{1,0:T(8,128)(2,1)}, u32[]{:S(2)}, u32[]{:S(2)}) %collective-permute-start.100) | collective-permute-done | bytes 1048608 | tf_op jit(solution)/shard_map/ppermute | solution.py:154
  120.3 20.3 %collective-permute-done.91.far_ref = bf16[256,2048]{1,0:T(8,128)(2,1)S(1)} collective-permute-done((bf16[256,2048]{1,0:T(8,128)(2,1)}, bf16[256,2048]{1,0:T(8,128)(2,1)S(1)}, u32[]{:S(2)}, u32[]{:S(2)}) %collective-permute-start.91) | collective-permute-done | bytes 1048608 | tf_op jit(solution)/shard_map/ppermute | solution.py:154
  142.7 20.4 %collective-permute-done.82.far_ref = bf16[256,2048]{1,0:T(8,128)(2,1)S(1)} collective-permute-done((bf16[256,2048]{1,0:T(8,128)(2,1)}, bf16[256,2048]{1,0:T(8,128)(2,1)S(1)}, u32[]{:S(2)}, u32[]{:S(2)}) %collective-permute-start.82) | collective-permute-done | bytes 1048608 | tf_op jit(solution)/shard_map/ppermute | solution.py:154
  165.5 20.2 %collective-permute-done.73.far_ref = bf16[256,2048]{1,0:T(8,128)(2,1)S(1)} collective-permute-done((bf16[256,2048]{1,0:T(8,128)(2,1)}, bf16[256,2048]{1,0:T(8,128)(2,1)S(1)}, u32[]{:S(2)}, u32[]{:S(2)}) %collective-permute-start.73) | collective-permute-done | bytes 1048608 | tf_op jit(solution)/shard_map/ppermute | solution.py:154
  187.7 20.4 %collective-permute-done.64.far_ref = bf16[256,2048]{1,0:T(8,128)(2,1)S(1)} collective-permute-done((bf16[256,2048]{1,0:T(8,128)(2,1)}, bf16[256,2048]{1,0:T(8,128)(2,1)S(1)}, u32[]{:S(2)}, u32[]{:S(2)}) %collective-permute-start.64) | collective-permute-done | bytes 1048608 | tf_op jit(solution)/shard_map/ppermute | solution.py:154
  210.2 20.4 %collective-permute-done.55.far_ref = bf16[256,2048]{1,0:T(8,128)(2,1)S(1)} collective-permute-done((bf16[256,2048]{1,0:T(8,128)(2,1)}, bf16[256,2048]{1,0:T(8,128)(2,1)S(1)}, u32[]{:S(2)}, u32[]{:S(2)}) %collective-permute-start.55) | collective-permute-done | bytes 1048608 | tf_op jit(solution)/shard_map/ppermute | solution.py:154
  232.6 20.6 %collective-permute-done.46.far_ref = bf16[256,2048]{1,0:T(8,128)(2,1)} collective-permute-done((bf16[256,2048]{1,0:T(8,128)(2,1)}, bf16[256,2048]{1,0:T(8,128)(2,1)}, u32[]{:S(2)}, u32[]{:S(2)}) %collective-permute-start.46) | collective-permute-done | bytes 1048608 | tf_op jit(solution)/shard_map/ppermute | solution.py:154
  258.4 17.3 %collective-permute-done.37.far_ref = bf16[256,2048]{1,0:T(8,128)(2,1)} collective-permute-done((bf16[256,2048]{1,0:T(8,128)(2,1)}, bf16[256,2048]{1,0:T(8,128)(2,1)}, u32[]{:S(2)}, u32[]{:S(2)}) %collective-permute-start.37) | collective-permute-done | bytes 1048608 | tf_op jit(solution)/shard_map/ppermute | solution.py:154
  283.7 14.4 %collective-permute-done.28.far_ref = bf16[256,2048]{1,0:T(8,128)(2,1)} collective-permute-done((bf16[256,2048]{1,0:T(8,128)(2,1)}, bf16[256,2048]{1,0:T(8,128)(2,1)}, u32[]{:S(2)}, u32[]{:S(2)}) %collective-permute-start.28) | collective-permute-done | bytes 1048608 | tf_op jit(solution)/shard_map/ppermute | solution.py:154
  300.1 20.4 %collective-permute-done.19.far_ref = bf16[256,2048]{1,0:T(8,128)(2,1)} collective-permute-done((bf16[256,2048]{1,0:T(8,128)(2,1)}, bf16[256,2048]{1,0:T(8,128)(2,1)}, u32[]{:S(2)}, u32[]{:S(2)}) %collective-permute-start.19) | collective-permute-done | bytes 1048608 | tf_op jit(solution)/shard_map/ppermute | solution.py:154
  328.6 14.3 %collective-permute-done.10.far_ref = bf16[256,2048]{1,0:T(8,128)(2,1)S(1)} collective-permute-done((bf16[256,2048]{1,0:T(8,128)(2,1)}, bf16[256,2048]{1,0:T(8,128)(2,1)S(1)}, u32[]{:S(2)}, u32[]{:S(2)}) %collective-permute-start.10) | collective-permute-done | bytes 1048608 | tf_op jit(solution)/shard_map/ppermute | solution.py:154
  345.0 19.6 %collective-permute-done.1.far_ref = bf16[256,2048]{1,0:T(8,128)(2,1)S(1)} collective-permute-done((bf16[256,2048]{1,0:T(8,128)(2,1)}, bf16[256,2048]{1,0:T(8,128)(2,1)S(1)}, u32[]{:S(2)}, u32[]{:S(2)}) %collective-permute-start.1) | collective-permute-done | bytes 1048608 | tf_op jit(solution)/shard_map/ppermute | solution.py:154
  395.7 17.7 %collective-permute-done.92.refs_0_ = bf16[256,2048]{1,0:T(8,128)(2,1)} collective-permute-done((bf16[256,2048]{1,0:T(8,128)(2,1)}, bf16[256,2048]{1,0:T(8,128)(2,1)}, u32[]{:S(2)}, u32[]{:S(2)}) %collective-permute-start.92) | collective-permute-done | bytes 1048608 | tf_op jit(solution)/shard_map/ppermute | solution.py:147
  421.2 14.7 %collective-permute-done.83.refs_0_ = bf16[256,2048]{1,0:T(8,128)(2,1)} collective-permute-done((bf16[256,2048]{1,0:T(8,128)(2,1)}, bf16[256,2048]{1,0:T(8,128)(2,1)}, u32[]{:S(2)}, u32[]{:S(2)}) %collective-permute-start.83) | collective-permute-done | bytes 1048608 | tf_op jit(solution)/shard_map/ppermute | solution.py:147
  437.6 20.6 %collective-permute-done.74.refs_0_ = bf16[256,2048]{1,0:T(8,128)(2,1)S(1)} collective-permute-done((bf16[256,2048]{1,0:T(8,128)(2,1)}, bf16[256,2048]{1,0:T(8,128)(2,1)S(1)}, u32[]{:S(2)}, u32[]{:S(2)}) %collective-permute-start.74) | collective-permute-done | bytes 1048608 | tf_op jit(solution)/shard_map/ppermute | solution.py:147
  466.0 14.7 %collective-permute-done.65.refs_0_ = bf16[256,2048]{1,0:T(8,128)(2,1)S(1)} collective-permute-done((bf16[256,2048]{1,0:T(8,128)(2,1)}, bf16[256,2048]{1,0:T(8,128)(2,1)S(1)}, u32[]{:S(2)}, u32[]{:S(2)}) %collective-permute-start.65) | collective-permute-done | bytes 1048608 | tf_op jit(solution)/shard_map/ppermute | solution.py:147
  482.4 20.7 %collective-permute-done.56.refs_0_ = bf16[256,2048]{1,0:T(8,128)(2,1)S(1)} collective-permute-done((bf16[256,2048]{1,0:T(8,128)(2,1)}, bf16[256,2048]{1,0:T(8,128)(2,1)S(1)}, u32[]{:S(2)}, u32[]{:S(2)}) %collective-permute-start.56) | collective-permute-done | bytes 1048608 | tf_op jit(solution)/shard_map/ppermute | solution.py:147
  507.9 17.8 %collective-permute-done.47.refs_0_ = bf16[256,2048]{1,0:T(8,128)(2,1)} collective-permute-done((bf16[256,2048]{1,0:T(8,128)(2,1)}, bf16[256,2048]{1,0:T(8,128)(2,1)}, u32[]{:S(2)}, u32[]{:S(2)}) %collective-permute-start.47) | collective-permute-done | bytes 1048608 | tf_op jit(solution)/shard_map/ppermute | solution.py:147
  530.8 17.4 %collective-permute-done.38.refs_0_ = bf16[256,2048]{1,0:T(8,128)(2,1)} collective-permute-done((bf16[256,2048]{1,0:T(8,128)(2,1)}, bf16[256,2048]{1,0:T(8,128)(2,1)}, u32[]{:S(2)}, u32[]{:S(2)}) %collective-permute-start.38) | collective-permute-done | bytes 1048608 | tf_op jit(solution)/shard_map/ppermute | solution.py:147
  548.2 22.5 %collective-permute-done.29.refs_0_ = bf16[256,2048]{1,0:T(8,128)(2,1)} collective-permute-done((bf16[256,2048]{1,0:T(8,128)(2,1)}, bf16[256,2048]{1,0:T(8,128)(2,1)}, u32[]{:S(2)}, u32[]{:S(2)}) %collective-permute-start.29) | collective-permute-done | bytes 1048608 | tf_op jit(solution)/shard_map/ppermute | solution.py:147
  572.5 20.5 %collective-permute-done.20.refs_0_ = bf16[256,2048]{1,0:T(8,128)(2,1)S(1)} collective-permute-done((bf16[256,2048]{1,0:T(8,128)(2,1)}, bf16[256,2048]{1,0:T(8,128)(2,1)S(1)}, u32[]{:S(2)}, u32[]{:S(2)}) %collective-permute-start.20) | collective-permute-done | bytes 1048608 | tf_op jit(solution)/shard_map/ppermute | solution.py:147
  593.0 22.5 %collective-permute-done.11.refs_0_ = bf16[256,2048]{1,0:T(8,128)(2,1)S(1)} collective-permute-done((bf16[256,2048]{1,0:T(8,128)(2,1)}, bf16[256,2048]{1,0:T(8,128)(2,1)S(1)}, u32[]{:S(2)}, u32[]{:S(2)}) %collective-permute-start.11) | collective-permute-done | bytes 1048608 | tf_op jit(solution)/shard_map/ppermute | solution.py:147
  618.3 18.0 %collective-permute-done.2.refs_0_ = bf16[256,2048]{1,0:T(8,128)(2,1)S(1)} collective-permute-done((bf16[256,2048]{1,0:T(8,128)(2,1)}, bf16[256,2048]{1,0:T(8,128)(2,1)S(1)}, u32[]{:S(2)}, u32[]{:S(2)}) %collective-permute-start.2) | collective-permute-done | bytes 1048608 | tf_op jit(solution)/shard_map/ppermute | solution.py:147
  666.1 8.1 collective-permute-done.133.refs_5_
  684.4 11.7 %collective-permute-done.123.refs_4_ = bf16[32,2048]{1,0:T(8,128)(2,1)S(1)} collective-permute-done((bf16[32,2048]{1,0:T(8,128)(2,1)S(1)}, bf16[32,2048]{1,0:T(8,128)(2,1)S(1)}, u32[]{:S(2)}, u32[]{:S(2)}) %collective-permute-start.123) | collective-permute-done | bytes 131104 | tf_op jit(solution)/shard_map/ppermute | solution.py:183
  780.1 7.7 collective-permute-done.88.refs_5_
  798.4 11.4 %collective-permute-done.78.refs_4_ = bf16[32,2048]{1,0:T(8,128)(2,1)S(1)} collective-permute-done((bf16[32,2048]{1,0:T(8,128)(2,1)S(1)}, bf16[32,2048]{1,0:T(8,128)(2,1)S(1)}, u32[]{:S(2)}, u32[]{:S(2)}) %collective-permute-start.78) | collective-permute-done | bytes 131104 | tf_op jit(solution)/shard_map/ppermute | solution.py:183
  846.8 8.2 collective-permute-done.60.refs_4_
  912.6 11.4 %collective-permute-done.33.refs_4_ = bf16[32,2048]{1,0:T(8,128)(2,1)} collective-permute-done((bf16[32,2048]{1,0:T(8,128)(2,1)S(1)}, bf16[32,2048]{1,0:T(8,128)(2,1)}, u32[]{:S(2)}, u32[]{:S(2)}) %collective-permute-start.33) | collective-permute-done | bytes 131104 | tf_op jit(solution)/shard_map/ppermute | solution.py:183
  960.7 8.3 collective-permute-done.15.refs_4_
  (602 shorter events, 495.3 us)
Async XLA Ops:
  9.0 96.3 %collective-permute-start.118 = (bf16[256,2048]{1,0:T(8,128)(2,1)}, bf16[256,2048]{1,0:T(8,128)(2,1)}, u32[]{:S(2)}, u32[]{:S(2)}) collective-permute-start(bf16[256,2048]{1,0:T(8,128)(2,1)} %slice.94), channel_id=1, source_target_pairs={{0,8},{8,0},{16,24},{24,16},{1,9},{9,1},{17,25},{25,17},{2,10},{10... | collective-permute-start | bytes 3145736 | tf_op jit(solution)/shard_map/ppermute | solution.py:154
  13.3 92.5 %collective-permute-start.109 = (bf16[256,2048]{1,0:T(8,128)(2,1)}, bf16[256,2048]{1,0:T(8,128)(2,1)S(1)}, u32[]{:S(2)}, u32[]{:S(2)}) collective-permute-start(bf16[256,2048]{1,0:T(8,128)(2,1)} %slice.95), channel_id=1, source_target_pairs={{0,8},{8,0},{16,24},{24,16},{1,9},{9,1},{17,25},{25,17},{2,10},{10... | collective-permute-start | bytes 3145736 | tf_op jit(solution)/shard_map/ppermute | solution.py:154
  23.3 95.0 %collective-permute-start.100 = (bf16[256,2048]{1,0:T(8,128)(2,1)}, bf16[256,2048]{1,0:T(8,128)(2,1)}, u32[]{:S(2)}, u32[]{:S(2)}) collective-permute-start(bf16[256,2048]{1,0:T(8,128)(2,1)} %slice.96), channel_id=1, source_target_pairs={{0,8},{8,0},{16,24},{24,16},{1,9},{9,1},{17,25},{25,17},{2,10},{10... | collective-permute-start | bytes 3145736 | tf_op jit(solution)/shard_map/ppermute | solution.py:154
  28.3 112.4 %collective-permute-start.91 = (bf16[256,2048]{1,0:T(8,128)(2,1)}, bf16[256,2048]{1,0:T(8,128)(2,1)S(1)}, u32[]{:S(2)}, u32[]{:S(2)}) collective-permute-start(bf16[256,2048]{1,0:T(8,128)(2,1)} %slice.97), channel_id=1, source_target_pairs={{0,8},{8,0},{16,24},{24,16},{1,9},{9,1},{17,25},{25,17},{2,10},{10... | collective-permute-start | bytes 3145736 | tf_op jit(solution)/shard_map/ppermute | solution.py:154
  50.9 112.2 %collective-permute-start.82 = (bf16[256,2048]{1,0:T(8,128)(2,1)}, bf16[256,2048]{1,0:T(8,128)(2,1)S(1)}, u32[]{:S(2)}, u32[]{:S(2)}) collective-permute-start(bf16[256,2048]{1,0:T(8,128)(2,1)} %slice.98), channel_id=1, source_target_pairs={{0,8},{8,0},{16,24},{24,16},{1,9},{9,1},{17,25},{25,17},{2,10},{10... | collective-permute-start | bytes 3145736 | tf_op jit(solution)/shard_map/ppermute | solution.py:154
  105.2 80.4 %collective-permute-start.73 = (bf16[256,2048]{1,0:T(8,128)(2,1)}, bf16[256,2048]{1,0:T(8,128)(2,1)S(1)}, u32[]{:S(2)}, u32[]{:S(2)}) collective-permute-start(bf16[256,2048]{1,0:T(8,128)(2,1)} %slice.99), channel_id=1, source_target_pairs={{0,8},{8,0},{16,24},{24,16},{1,9},{9,1},{17,25},{25,17},{2,10},{10... | collective-permute-start | bytes 3145736 | tf_op jit(solution)/shard_map/ppermute | solution.py:154
  105.8 102.3 %collective-permute-start.64 = (bf16[256,2048]{1,0:T(8,128)(2,1)}, bf16[256,2048]{1,0:T(8,128)(2,1)S(1)}, u32[]{:S(2)}, u32[]{:S(2)}) collective-permute-start(bf16[256,2048]{1,0:T(8,128)(2,1)} %slice.100), channel_id=1, source_target_pairs={{0,8},{8,0},{16,24},{24,16},{1,9},{9,1},{17,25},{25,17},{2,10},{10... | collective-permute-start | bytes 3145736 | tf_op jit(solution)/shard_map/ppermute | solution.py:154
  118.3 112.2 %collective-permute-start.55 = (bf16[256,2048]{1,0:T(8,128)(2,1)}, bf16[256,2048]{1,0:T(8,128)(2,1)S(1)}, u32[]{:S(2)}, u32[]{:S(2)}) collective-permute-start(bf16[256,2048]{1,0:T(8,128)(2,1)} %slice.101), channel_id=1, source_target_pairs={{0,8},{8,0},{16,24},{24,16},{1,9},{9,1},{17,25},{25,17},{2,10},{10... | collective-permute-start | bytes 3145736 | tf_op jit(solution)/shard_map/ppermute | solution.py:154
  140.7 112.5 %collective-permute-start.46 = (bf16[256,2048]{1,0:T(8,128)(2,1)}, bf16[256,2048]{1,0:T(8,128)(2,1)}, u32[]{:S(2)}, u32[]{:S(2)}) collective-permute-start(bf16[256,2048]{1,0:T(8,128)(2,1)} %slice.102), channel_id=1, source_target_pairs={{0,8},{8,0},{16,24},{24,16},{1,9},{9,1},{17,25},{25,17},{2,10},{10... | collective-permute-start | bytes 3145736 | tf_op jit(solution)/shard_map/ppermute | solution.py:154
  163.2 112.5 %collective-permute-start.37 = (bf16[256,2048]{1,0:T(8,128)(2,1)}, bf16[256,2048]{1,0:T(8,128)(2,1)}, u32[]{:S(2)}, u32[]{:S(2)}) collective-permute-start(bf16[256,2048]{1,0:T(8,128)(2,1)} %slice.103), channel_id=1, source_target_pairs={{0,8},{8,0},{16,24},{24,16},{1,9},{9,1},{17,25},{25,17},{2,10},{10... | collective-permute-start | bytes 3145736 | tf_op jit(solution)/shard_map/ppermute | solution.py:154
  185.6 112.5 %collective-permute-start.28 = (bf16[256,2048]{1,0:T(8,128)(2,1)}, bf16[256,2048]{1,0:T(8,128)(2,1)}, u32[]{:S(2)}, u32[]{:S(2)}) collective-permute-start(bf16[256,2048]{1,0:T(8,128)(2,1)} %slice.104), channel_id=1, source_target_pairs={{0,8},{8,0},{16,24},{24,16},{1,9},{9,1},{17,25},{25,17},{2,10},{10... | collective-permute-start | bytes 3145736 | tf_op jit(solution)/shard_map/ppermute | solution.py:154
  208.1 112.5 %collective-permute-start.19 = (bf16[256,2048]{1,0:T(8,128)(2,1)}, bf16[256,2048]{1,0:T(8,128)(2,1)}, u32[]{:S(2)}, u32[]{:S(2)}) collective-permute-start(bf16[256,2048]{1,0:T(8,128)(2,1)} %slice.105), channel_id=1, source_target_pairs={{0,8},{8,0},{16,24},{24,16},{1,9},{9,1},{17,25},{25,17},{2,10},{10... | collective-permute-start | bytes 3145736 | tf_op jit(solution)/shard_map/ppermute | solution.py:154
  230.6 112.4 %collective-permute-start.10 = (bf16[256,2048]{1,0:T(8,128)(2,1)}, bf16[256,2048]{1,0:T(8,128)(2,1)S(1)}, u32[]{:S(2)}, u32[]{:S(2)}) collective-permute-start(bf16[256,2048]{1,0:T(8,128)(2,1)} %slice.106), channel_id=1, source_target_pairs={{0,8},{8,0},{16,24},{24,16},{1,9},{9,1},{17,25},{25,17},{2,10},{10... | collective-permute-start | bytes 3145736 | tf_op jit(solution)/shard_map/ppermute | solution.py:154
  253.2 111.4 %collective-permute-start.1 = (bf16[256,2048]{1,0:T(8,128)(2,1)}, bf16[256,2048]{1,0:T(8,128)(2,1)S(1)}, u32[]{:S(2)}, u32[]{:S(2)}) collective-permute-start(bf16[256,2048]{1,0:T(8,128)(2,1)} %slice.107), channel_id=1, source_target_pairs={{0,8},{8,0},{16,24},{24,16},{1,9},{9,1},{17,25},{25,17},{2,10},{10... | collective-permute-start | bytes 3145736 | tf_op jit(solution)/shard_map/ppermute | solution.py:154
  275.6 93.7 %collective-permute-start.137 = (bf16[256,2048]{1,0:T(8,128)(2,1)}, bf16[256,2048]{1,0:T(8,128)(2,1)}, u32[]{:S(2)}, u32[]{:S(2)}) collective-permute-start(bf16[256,2048]{1,0:T(8,128)(2,1)} %shard_map.85), channel_id=1, source_target_pairs={{0,16},{8,24},{16,0},{24,8},{1,17},{9,25},{17,1},{25,9},{2,18},{10... | collective-permute-start | bytes 3145736 | tf_op jit(solution)/shard_map/ppermute | solution.py:147
  298.1 77.7 %collective-permute-start.128 = (bf16[256,2048]{1,0:T(8,128)(2,1)S(1)}, bf16[256,2048]{1,0:T(8,128)(2,1)}, u32[]{:S(2)}, u32[]{:S(2)}) collective-permute-start(bf16[256,2048]{1,0:T(8,128)(2,1)S(1)} %copy-done.16), channel_id=1, source_target_pairs={{0,16},{8,24},{16,0},{24,8},{1,17},{9,25},{17,1},{25,9},{2,18},{10... | collective-permute-start | bytes 3145736 | tf_op jit(solution)/shard_map/ppermute | solution.py:147
  375.8 60.1 %collective-permute-start.83 = (bf16[256,2048]{1,0:T(8,128)(2,1)}, bf16[256,2048]{1,0:T(8,128)(2,1)}, u32[]{:S(2)}, u32[]{:S(2)}) collective-permute-start(bf16[256,2048]{1,0:T(8,128)(2,1)} %shard_map.73), channel_id=1, source_target_pairs={{0,16},{8,24},{16,0},{24,8},{1,17},{9,25},{17,1},{25,9},{2,18},{10... | collective-permute-start | bytes 3145736 | tf_op jit(solution)/shard_map/ppermute | solution.py:147
  377.4 80.8 %collective-permute-start.74 = (bf16[256,2048]{1,0:T(8,128)(2,1)}, bf16[256,2048]{1,0:T(8,128)(2,1)S(1)}, u32[]{:S(2)}, u32[]{:S(2)}) collective-permute-start(bf16[256,2048]{1,0:T(8,128)(2,1)} %shard_map.71), channel_id=1, source_target_pairs={{0,16},{8,24},{16,0},{24,8},{1,17},{9,25},{17,1},{25,9},{2,18},{10... | collective-permute-start | bytes 3145736 | tf_op jit(solution)/shard_map/ppermute | solution.py:147
  383.8 96.9 %collective-permute-start.65 = (bf16[256,2048]{1,0:T(8,128)(2,1)}, bf16[256,2048]{1,0:T(8,128)(2,1)S(1)}, u32[]{:S(2)}, u32[]{:S(2)}) collective-permute-start(bf16[256,2048]{1,0:T(8,128)(2,1)} %shard_map.69), channel_id=1, source_target_pairs={{0,16},{8,24},{16,0},{24,8},{1,17},{9,25},{17,1},{25,9},{2,18},{10... | collective-permute-start | bytes 3145736 | tf_op jit(solution)/shard_map/ppermute | solution.py:147
  390.9 112.2 %collective-permute-start.56 = (bf16[256,2048]{1,0:T(8,128)(2,1)}, bf16[256,2048]{1,0:T(8,128)(2,1)S(1)}, u32[]{:S(2)}, u32[]{:S(2)}) collective-permute-start(bf16[256,2048]{1,0:T(8,128)(2,1)} %shard_map.67), channel_id=1, source_target_pairs={{0,16},{8,24},{16,0},{24,8},{1,17},{9,25},{17,1},{25,9},{2,18},{10... | collective-permute-start | bytes 3145736 | tf_op jit(solution)/shard_map/ppermute | solution.py:147
  413.4 112.4 %collective-permute-start.47 = (bf16[256,2048]{1,0:T(8,128)(2,1)}, bf16[256,2048]{1,0:T(8,128)(2,1)}, u32[]{:S(2)}, u32[]{:S(2)}) collective-permute-start(bf16[256,2048]{1,0:T(8,128)(2,1)} %shard_map.65), channel_id=1, source_target_pairs={{0,16},{8,24},{16,0},{24,8},{1,17},{9,25},{17,1},{25,9},{2,18},{10... | collective-permute-start | bytes 3145736 | tf_op jit(solution)/shard_map/ppermute | solution.py:147
  435.8 112.4 %collective-permute-start.38 = (bf16[256,2048]{1,0:T(8,128)(2,1)}, bf16[256,2048]{1,0:T(8,128)(2,1)}, u32[]{:S(2)}, u32[]{:S(2)}) collective-permute-start(bf16[256,2048]{1,0:T(8,128)(2,1)} %shard_map.63), channel_id=1, source_target_pairs={{0,16},{8,24},{16,0},{24,8},{1,17},{9,25},{17,1},{25,9},{2,18},{10... | collective-permute-start | bytes 3145736 | tf_op jit(solution)/shard_map/ppermute | solution.py:147
  458.2 112.5 %collective-permute-start.29 = (bf16[256,2048]{1,0:T(8,128)(2,1)}, bf16[256,2048]{1,0:T(8,128)(2,1)}, u32[]{:S(2)}, u32[]{:S(2)}) collective-permute-start(bf16[256,2048]{1,0:T(8,128)(2,1)} %shard_map.61), channel_id=1, source_target_pairs={{0,16},{8,24},{16,0},{24,8},{1,17},{9,25},{17,1},{25,9},{2,18},{10... | collective-permute-start | bytes 3145736 | tf_op jit(solution)/shard_map/ppermute | solution.py:147
  480.7 112.4 %collective-permute-start.20 = (bf16[256,2048]{1,0:T(8,128)(2,1)}, bf16[256,2048]{1,0:T(8,128)(2,1)S(1)}, u32[]{:S(2)}, u32[]{:S(2)}) collective-permute-start(bf16[256,2048]{1,0:T(8,128)(2,1)} %shard_map.59), channel_id=1, source_target_pairs={{0,16},{8,24},{16,0},{24,8},{1,17},{9,25},{17,1},{25,9},{2,18},{10... | collective-permute-start | bytes 3145736 | tf_op jit(solution)/shard_map/ppermute | solution.py:147
  503.1 112.4 %collective-permute-start.11 = (bf16[256,2048]{1,0:T(8,128)(2,1)}, bf16[256,2048]{1,0:T(8,128)(2,1)S(1)}, u32[]{:S(2)}, u32[]{:S(2)}) collective-permute-start(bf16[256,2048]{1,0:T(8,128)(2,1)} %shard_map.57), channel_id=1, source_target_pairs={{0,16},{8,24},{16,0},{24,8},{1,17},{9,25},{17,1},{25,9},{2,18},{10... | collective-permute-start | bytes 3145736 | tf_op jit(solution)/shard_map/ppermute | solution.py:147
  525.7 110.6 %collective-permute-start.2 = (bf16[256,2048]{1,0:T(8,128)(2,1)}, bf16[256,2048]{1,0:T(8,128)(2,1)S(1)}, u32[]{:S(2)}, u32[]{:S(2)}) collective-permute-start(bf16[256,2048]{1,0:T(8,128)(2,1)} %shard_map.55), channel_id=1, source_target_pairs={{0,16},{8,24},{16,0},{24,8},{1,17},{9,25},{17,1},{25,9},{2,18},{10... | collective-permute-start | bytes 3145736 | tf_op jit(solution)/shard_map/ppermute | solution.py:147
  548.2 88.6 %collective-permute-start.138 = (bf16[32,2048]{1,0:T(8,128)(2,1)}, bf16[32,2048]{1,0:T(8,128)(2,1)S(1)}, u32[]{:S(2)}, u32[]{:S(2)}) collective-permute-start(bf16[32,2048]{1,0:T(8,128)(2,1)} %get-tuple-element.316), channel_id=1, source_target_pairs={{0,1},{1,0},{2,3},{3,2},{4,5},{5,4},{6,7},{7,6},{8,9},{9,8},{10,11... | collective-permute-start | bytes 393224 | tf_op jit(solution)/shard_map/ppermute | solution.py:183
  570.7 69.4 %collective-permute-start.139 = (bf16[32,2048]{1,0:T(8,128)(2,1)}, bf16[32,2048]{1,0:T(8,128)(2,1)S(1)}, u32[]{:S(2)}, u32[]{:S(2)}) collective-permute-start(bf16[32,2048]{1,0:T(8,128)(2,1)} %get-tuple-element.317), channel_id=1, source_target_pairs={{0,2},{1,3},{2,0},{3,1},{4,6},{5,7},{6,4},{7,5},{8,10},{9,11},{10,... | collective-permute-start | bytes 393224 | tf_op jit(solution)/shard_map/ppermute | solution.py:183
  971.1 66.1 %collective-permute-start.5 = (bf16[32,2048]{1,0:T(8,128)(2,1)}, bf16[32,2048]{1,0:T(8,128)(2,1)}, u32[]{:S(2)}, u32[]{:S(2)}) collective-permute-start(bf16[32,2048]{1,0:T(8,128)(2,1)} %get-tuple-element.183), channel_id=1, source_target_pairs={{0,3},{1,2},{2,1},{3,0},{4,7},{5,6},{6,5},{7,4},{8,11},{9,10},{10,... | collective-permute-start | bytes 393224 | tf_op jit(solution)/shard_map/ppermute | solution.py:183
  971.1 66.1 %collective-permute-start.6 = (bf16[32,2048]{1,0:T(8,128)(2,1)}, bf16[32,2048]{1,0:T(8,128)(2,1)}, u32[]{:S(2)}, u32[]{:S(2)}) collective-permute-start(bf16[32,2048]{1,0:T(8,128)(2,1)} %get-tuple-element.184), channel_id=1, source_target_pairs={{0,4},{1,5},{2,6},{3,7},{4,0},{5,1},{6,2},{7,3},{8,12},{9,13},{10,... | collective-permute-start | bytes 393224 | tf_op jit(solution)/shard_map/ppermute | solution.py:183
  975.7 61.5 %collective-permute-start.7 = (bf16[32,2048]{1,0:T(8,128)(2,1)}, bf16[32,2048]{1,0:T(8,128)(2,1)}, u32[]{:S(2)}, u32[]{:S(2)}) collective-permute-start(bf16[32,2048]{1,0:T(8,128)(2,1)} %get-tuple-element.185), channel_id=1, source_target_pairs={{0,5},{1,4},{2,7},{3,6},{4,1},{5,0},{6,3},{7,2},{8,13},{9,12},{10,... | collective-permute-start | bytes 393224 | tf_op jit(solution)/shard_map/ppermute | solution.py:183
  978.0 59.3 %collective-permute-start.8 = (bf16[32,2048]{1,0:T(8,128)(2,1)}, bf16[32,2048]{1,0:T(8,128)(2,1)}, u32[]{:S(2)}, u32[]{:S(2)}) collective-permute-start(bf16[32,2048]{1,0:T(8,128)(2,1)} %get-tuple-element.186), channel_id=1, source_target_pairs={{0,6},{1,7},{2,4},{3,5},{4,2},{5,3},{6,0},{7,1},{8,14},{9,15},{10,... | collective-permute-start | bytes 393224 | tf_op jit(solution)/shard_map/ppermute | solution.py:183
  (243 other events, 6309.5 us)

commit v2 on v0

v2 whole, which is shorter than its diff:
```python
import functools

import jax
import jax.numpy as jnp
from jax import lax
from jax.experimental import pallas as pl
from jax.experimental.pallas import tpu as pltpu
from jax.sharding import PartitionSpec as P

UNITS = 3
TILES = 2
AHEAD = 2
LAG = 4
VMEM = 67_000_000


def pair_energy(pairs, occ_energy):
    count = occ_energy.shape[0]
    first = pairs // count
    second = pairs % count
    grid = jnp.arange(count, dtype=jnp.int32)
    e_first = jnp.sum(jnp.where(first[:, None] == grid[None, :], occ_energy[None, :], 0.0), axis=1)
    e_second = jnp.sum(
        jnp.where(second[:, None] == grid[None, :], occ_energy[None, :], 0.0), axis=1
    )
    return e_first + e_second


def chunks_of(cols, virt):
    step = UNITS * virt
    return [(start, min(step, cols - start)) for start in range(0, cols, step)]


class Contract:
    def __init__(self, panel, which, own, far, start, extra=(), blocks=False, ahead=None):
        self.which, self.start, self.blocks, self.ahead = which, start, blocks, ahead
        self.n_extra = len(extra)
        self.n_col, _, self.per_dev, self.depth2 = panel.shape
        self.depth, self.width = far.shape
        self.rows = self.n_col * self.per_dev
        tiles = TILES + blocks
        self.tiles = tiles if self.width % (tiles * 128) == 0 else TILES if self.width % (TILES * 128) == 0 else 1
        self.tile = self.width // self.tiles
        self.ins = [panel, own, far, *extra]
        self.in_specs = [pl.BlockSpec(memory_space=pl.ANY)] * len(self.ins)
        bf16 = jnp.bfloat16
        pieces, share = (self.n_col // 2, 2 * self.per_dev) if blocks else (len(which), self.rows)
        self.pieces = pieces
        self.out_shape = [jax.ShapeDtypeStruct((share, self.width), bf16)] * pieces
        self.scratch = [
            pltpu.VMEM((len(which), self.n_col, self.per_dev, self.depth2), bf16),
            pltpu.VMEM((2, self.depth, self.width), bf16),
            pltpu.VMEM((max(self.n_extra, 1), self.rows, self.width), bf16),
            pltpu.VMEM((pieces, share, self.width), bf16),
            pltpu.SemaphoreType.DMA((len(which),)),
            pltpu.SemaphoreType.DMA((2 + self.n_extra, self.tiles)),
            pltpu.SemaphoreType.DMA((pieces, self.tiles)),
        ]
        if ahead:
            self.out_shape.append(jax.ShapeDtypeStruct((self.depth, ahead[1]), bf16))
            self.scratch += [pltpu.VMEM((self.depth, ahead[1]), bf16), pltpu.SemaphoreType.DMA((2,))]
        self.flops = 2 * self.rows * self.depth2 * self.width * len(which)
        self.bytes = 2 * self.width * (self.depth2 + self.rows * (len(which) + self.n_extra))

    def bind(self, ins, outs, scratch):
        (self.panel, self.own, self.far), self.extra = ins[:3], ins[3:]
        self.outs = outs[: self.pieces]
        self.t_buf, self.in_buf, self.extra_buf, self.out_buf = scratch[:4]
        self.t_sem, self.in_sem, self.out_sem = scratch[4:7]
        if self.ahead:
            self.later, (self.ahead_buf, self.ahead_sem) = outs[self.pieces], scratch[7:]

    def loads(self, i):
        at = pl.multiple_of(i * self.tile, 128)
        here = pl.ds(at, self.tile)
        there = pl.ds(pl.multiple_of(self.start + at, 128), self.tile)
        pairs = [(self.own.at[:, there], self.in_buf.at[0, :, here]), (self.far.at[:, here], self.in_buf.at[1, :, here])]
        pairs += [(ref.at[:, here], self.extra_buf.at[e, :, here]) for e, ref in enumerate(self.extra)]
        return [pltpu.make_async_copy(a, b, self.in_sem.at[e, i]) for e, (a, b) in enumerate(pairs)]

    def stores(self, i):
        here = pl.ds(pl.multiple_of(i * self.tile, 128), self.tile)
        return [
            pltpu.make_async_copy(self.out_buf.at[m, :, here], ref.at[:, here], self.out_sem.at[m, i])
            for m, ref in enumerate(self.outs)
        ]

    def panels(self):
        return [
            pltpu.make_async_copy(self.panel.at[:, d], self.t_buf.at[q], self.t_sem.at[q])
            for q, d in enumerate(self.which)
        ]

    def ahead_load(self):
        start, width = self.ahead
        return pltpu.make_async_copy(self.own.at[:, pl.ds(start, width)], self.ahead_buf, self.ahead_sem.at[0])

    def ahead_store(self):
        return pltpu.make_async_copy(self.ahead_buf, self.later, self.ahead_sem.at[1])

    def begin(self):
        for copy in self.panels():
            copy.start()
        for i in range(self.tiles):
            for copy in self.loads(i):
                copy.start()
        if self.ahead:
            self.ahead_load().start()

    def run(self):
        for copy in self.panels():
            copy.wait()
        ts = [
            jnp.concatenate([self.t_buf[q, m] for m in range(self.n_col)], axis=0)
            for q in range(len(self.which))
        ]

        @pl.loop(0, self.tiles)
        def _(i):
            for copy in self.loads(i):
                copy.wait()
            here = pl.ds(pl.multiple_of(i * self.tile, 128), self.tile)
            for q, t in enumerate(ts):
                acc = jnp.dot(t[:, : self.depth], self.in_buf[0, :, here], preferred_element_type=jnp.float32)
                acc += jnp.dot(t[:, self.depth :], self.in_buf[1, :, here], preferred_element_type=jnp.float32)
                for e in range(self.n_extra):
                    acc += self.extra_buf[e, :, here].astype(jnp.float32)
                if self.blocks:
                    share = 2 * self.per_dev
                    for m in range(self.pieces):
                        rows = acc[m * share : (m + 1) * share]
                        self.out_buf[m, :, here] = rows.astype(self.out_buf.dtype)
                else:
                    self.out_buf[q, :, here] = acc.astype(self.out_buf.dtype)
            for copy in self.stores(i):
                copy.start()

        if self.ahead:
            self.ahead_load().wait()
            self.ahead_store().start()

    def end(self):
        for i in range(self.tiles):
            for copy in self.stores(i):
                copy.wait()
        if self.ahead:
            self.ahead_store().wait()


class Update:
    def __init__(self, old, other, moved, source, energy, virt_energy, start, out):
        self.start, self.prev, self.host = start, out, None
        if isinstance(out, Update):
            self.prev, self.host = None, out
        rows, columns = old.shape
        self.n_col, self.width = len(moved), moved[0].shape[1]
        self.cols, self.rows, self.virt = columns // self.n_col, rows, virt_energy.shape[0]
        self.ins = [source, virt_energy, energy, virt_energy[None, :], old, other, *moved]
        self.in_specs = [
            pl.BlockSpec(memory_space=pltpu.SMEM),
            pl.BlockSpec(memory_space=pltpu.SMEM),
            pl.BlockSpec(memory_space=pltpu.VMEM),
            pl.BlockSpec(memory_space=pltpu.VMEM),
        ] + [pl.BlockSpec(memory_space=pl.ANY)] * (2 + self.n_col)
        if self.prev is not None:
            self.ins.append(out)
            self.in_specs.append(pl.BlockSpec(memory_space=pl.ANY))
        self.out_shape = [] if self.host else [jax.ShapeDtypeStruct((rows, columns), old.dtype)]
        self.scratch = [pltpu.VMEM((self.n_col, rows, self.width), jnp.bfloat16)] * 4 + [
            pltpu.SemaphoreType.DMA((3, self.n_col)),
            pltpu.SemaphoreType.DMA((self.n_col,)),
        ]
        self.flops = 8 * self.n_col * rows * self.width
        self.bytes = 8 * self.n_col * rows * self.width

    def bind(self, ins, outs, scratch):
        self.source, self.va, self.e, self.vb, self.old, self.other = ins[:6]
        self.moved = ins[6 : 6 + self.n_col]
        self.out = self.host.out if self.host else outs[0]
        self.old_buf, self.other_buf, self.moved_buf, self.new_buf, self.in_sem, self.out_sem = scratch

    def place(self, m):
        return pl.ds(pl.multiple_of(self.source[m] * self.cols + self.start, 128), self.width)

    def loads(self, m):
        return [
            pltpu.make_async_copy(self.old.at[:, self.place(m)], self.old_buf.at[m], self.in_sem.at[0, m]),
            pltpu.make_async_copy(self.other.at[:, self.place(m)], self.other_buf.at[m], self.in_sem.at[1, m]),
        ]

    def arrive(self, m, which):
        rows = pl.ds(which % 2 * self.rows, self.rows)
        return pltpu.make_async_copy(self.moved[which].at[rows], self.moved_buf.at[m], self.in_sem.at[2, m])

    def store(self, m):
        return pltpu.make_async_copy(self.new_buf.at[m], self.out.at[:, self.place(m)], self.out_sem.at[m])

    def begin(self):
        for m in range(self.n_col):
            self.arrive(m, m).start()

        @pl.loop(0, self.n_col)
        def _(m):
            for copy in self.loads(m):
                copy.start()

    def run(self):
        virt = self.virt
        energy = jnp.broadcast_to(self.e[...], (self.rows, virt))

        @pl.loop(0, self.n_col)
        def _(m):
            for copy in [*self.loads(m), self.arrive(m, 0)]:
                copy.wait()
            first = (self.source[m] * self.cols + self.start) // virt

            @pl.loop(0, self.width // virt)
            def _(s):
                part = pl.ds(pl.multiple_of(s * virt, 128), virt)
                inverse = 1.0 / (energy - (self.va[first + s] + self.vb[...]))
                top = self.other_buf[m, :, part].astype(jnp.float32) + self.moved_buf[m, :, part].astype(jnp.float32)
                new = self.old_buf[m, :, part].astype(jnp.float32) + top * inverse
                self.new_buf[m, :, part] = new.astype(self.new_buf.dtype)

            self.store(m).start()

    def end(self):
        @pl.loop(0, self.n_col)
        def _(m):
            self.store(m).wait()


def kernel(jobs, *refs):
    refs = list(refs)
    take = lambda n: [refs.pop(0) for _ in range(n)]
    ins = [take(len(job.ins)) for job in jobs]
    outs = [take(len(job.out_shape)) for job in jobs]
    for job, job_ins, job_outs in zip(jobs, ins, outs):
        job.bind(job_ins, job_outs, take(len(job.scratch)))
    for job in jobs:
        job.begin()
    for job in jobs:
        job.run()
    for job in jobs:
        job.end()


def call(*jobs):
    jobs = [job for job in jobs if job is not None]
    alias, n_in, n_out = {}, 0, 0
    for job in jobs:
        n_in += len(job.ins)
        if getattr(job, "prev", None) is not None:
            alias[n_in - 1] = n_out
        n_out += len(job.out_shape)
    flat = lambda name: [x for job in jobs for x in getattr(job, name)]
    results = pl.pallas_call(
        functools.partial(kernel, jobs),
        in_specs=flat("in_specs"),
        out_specs=[pl.BlockSpec(memory_space=pl.ANY)] * n_out,
        out_shape=flat("out_shape"),
        scratch_shapes=flat("scratch"),
        input_output_aliases=alias,
        compiler_params=pltpu.CompilerParams(vmem_limit_bytes=VMEM),
        cost_estimate=pl.CostEstimate(
            flops=sum(job.flops for job in jobs),
            bytes_accessed=sum(job.bytes for job in jobs),
            transcendentals=0,
        ),
    )(*flat("ins"))
    results = list(results)
    return [[results.pop(0) for _ in job.out_shape] for job in jobs]


def local(amps_old, other_terms, occ_energy, virt_energy, integrals):
    n_row = lax.axis_size("row")
    n_col = lax.axis_size("col")
    row_id = lax.axis_index("row")
    col_id = lax.axis_index("col")
    per_dev = amps_old.shape[0]
    depth, cols = integrals.shape
    n_hi = n_row // 2
    hi, lo = row_id // 2, row_id % 2
    chunks = chunks_of(cols, virt_energy.shape[0])
    count = len(chunks)
    swap = [(r, r ^ 1) for r in range(n_row)]

    def shift(value, d):
        perm = [(r, ((r // 2 + d) % n_hi) * 2 + r % 2) for r in range(n_row)]
        return lax.ppermute(value, "row", perm)

    def trade(value, m):
        return lax.ppermute(value, "col", [(c, c ^ m) for c in range(n_col)])

    far = {}

    def fetch(k, piece):
        far[k] = lax.ppermute(piece, "row", swap)

    whole = integrals
    for k, (start, width) in enumerate(chunks[:AHEAD]):
        piece = whole[:, start : start + width]
        whole, piece = lax.optimization_barrier((whole, piece))
        fetch(k, piece)

    def pick(g):
        groups = [g * 2 + lo, g * 2 + 1 - lo]
        window = amps_old[:, : depth * n_row]
        return jnp.concatenate([lax.dynamic_slice_in_dim(window, q * depth, depth, 1) for q in groups], axis=1)

    mine = [pick(hi)]
    for d in range(1, n_hi):
        mine.append(shift(pick((hi - d) % n_hi), -d))
    panel = jnp.stack(mine)[None]
    step = n_col // 2
    while step:
        panel = jnp.stack([panel, trade(panel, step)], axis=1).reshape(-1, *panel.shape[1:])
        step //= 2
    source = col_id ^ jnp.arange(n_col, dtype=jnp.int32)

    first_pair = (row_id * n_col + col_id) * per_dev
    energy = pair_energy(first_pair + jnp.arange(per_dev, dtype=jnp.int32), occ_energy)[:, None]

    moved = {}
    out = None

    def renew(k, onto):
        start = chunks[k][0]
        return Update(amps_old, other_terms, moved[k], source, energy, virt_energy, start, onto)

    for k, (start, width) in enumerate(chunks):
        ahead = chunks[k + AHEAD] if k + AHEAD < count else None
        job = Contract(panel, range(1, n_hi), integrals, far[k], start, ahead=ahead)
        if k >= LAG:
            parts, (out,) = call(job, renew(k - LAG, out))
        else:
            (parts,) = call(job)
        if ahead:
            fetch(k + AHEAD, parts.pop())
        got = [shift(part, d) for d, part in enumerate(parts, 1)]
        (ladder,) = call(Contract(panel, (0,), integrals, far[k], start, got, blocks=True))
        moved[k] = []
        for m, block in enumerate(ladder):
            if m:
                block = trade(block, 2 * m)
            moved[k] += [block, trade(block, 1)]
    for k in (count - 4, count - 3):
        ((out,),) = call(renew(k, out))
    first = renew(count - 2, out)
    (out,), _ = call(first, renew(count - 1, first))
    return out


def solution(mesh):
    return jax.shard_map(
        local,
        mesh=mesh,
        in_specs=(P(("row", "col"), None), P(("row", "col"), None), P(), P(), P("row", "col")),
        out_specs=P(("row", "col"), None),
        check_vma=False,
    )
```

time: 1050 us -> 662 us (0.63)
  waiting for transfers between devices: 921 us -> 263 us
  starting transfers between devices: 5.75 us -> 197 us
  Pallas kernels: 0 us -> 191 us
  other arithmetic: 36.5 us -> 0.79 us
  matrix products: 30.6 us -> 0 us
  blocking collectives: 29 us -> 0 us
  between operations: 13.5 us -> 1.13 us
    unnamed x2 -> x0, waiting for transfers between devices: 558 us -> none
    all_to_all x1 -> x0, waiting for transfers between devices: 363 us -> none  [local(): lax.all_to_all(ladder.astype(jnp.bfloat16), 'col', split_axis=0, concat_a...]
    ppermute x0 -> x202, waiting for transfers between devices: none -> 263 us  [the longest x157 139 us: trade(): return lax.ppermute(value, 'col', [(c, c ^ m) for c in range(n_col)])]
    ppermute x0 -> x202, starting transfers between devices: none -> 197 us  [the longest x157 141 us: trade(): return lax.ppermute(value, 'col', [(c, c ^ m) for c in range(n_col)])]
    pallas_call x0 -> x47, Pallas kernels: none -> 191 us  [call(): pl.pallas_call(functools.partial(kernel, jobs), in_specs=flat('in_specs')...]
    dot_general x1 -> x0, matrix products: 30.6 us -> none  [local(): jnp.dot(panel, integrals, preferred_element_type=jnp.float32)]
    convert_element_type x1 -> x0, other arithmetic: 27.6 us -> none  [local(): return updated.astype(jnp.bfloat16)]
    all_gather x1 -> x0, blocking collectives: 16.5 us -> none  [local(): row_pairs = lax.all_gather(window, 'col', axis=0, tiled=True)]
  transfers between devices with their start and end apart: 2 -> 202, of which waited for: 2 -> 61; matrix products, arithmetic and copies ran while one was open for 0% -> 1% of each run, Pallas kernels for 0% -> 28%
where the time goes in v2:
time: 662 us; the launch traced here: 658 us
  waiting for transfers between devices  263 us (40%)
  starting transfers between devices  197 us (30%)
  Pallas kernels  191 us (29%)
    pallas_call x47, Pallas kernels, call(): pl.pallas_call(functools.partial(kernel, jobs), in_specs=flat('in_specs')...  191 us
    ppermute x157, starting transfers between devices, trade(): return lax.ppermute(value, 'col', [(c, c ^ m) for c in range(n_col)])  141 us
    ppermute x157, waiting for transfers between devices, trade(): return lax.ppermute(value, 'col', [(c, c ^ m) for c in range(n_col)])  139 us
    ppermute x22, waiting for transfers between devices, fetch(): far[k] = lax.ppermute(piece, 'row', swap)  94.6 us
    ppermute x23, waiting for transfers between devices, shift(): return lax.ppermute(value, 'row', perm)  29.2 us
    ppermute x22, starting transfers between devices, fetch(): far[k] = lax.ppermute(piece, 'row', swap)  29.1 us
    ppermute x23, starting transfers between devices, shift(): return lax.ppermute(value, 'row', perm)  26.3 us
  transfers between devices with their start and end apart: 202, of which 61 were waited for; matrix products, arithmetic and copies ran while one was open for 1% of the time, Pallas kernels for 28%

profile of v2, /device:TPU:0, one launch (start us, length us, event | category | flops | bytes accessed | tf_op | source)
XLA Modules:
  0.0 658.4 jit_solution(8497292640819789591)
XLA Ops:
  21.9 8.8 %collective-permute-done.4.refs_2_ = bf16[256,1536]{1,0:T(8,128)(2,1)} collective-permute-done((bf16[256,1536]{1,0:T(8,128)(2,1)S(1)}, bf16[256,1536]{1,0:T(8,128)(2,1)}, u32[]{:S(2)}, u32[]{:S(2)}) %collective-permute-start.4) | collective-permute-done | bytes 786464 | tf_op jit(solution)/shard_map/ppermute | solution.py:298
  37.1 10.5 %collective-permute-done.24.refs_2_ = bf16[256,1536]{1,0:T(8,128)(2,1)} collective-permute-done((bf16[256,1536]{1,0:T(8,128)(2,1)}, bf16[256,1536]{1,0:T(8,128)(2,1)}, u32[]{:S(2)}, u32[]{:S(2)}) %collective-permute-start.24) | collective-permute-done | bytes 786464 | tf_op jit(solution)/shard_map/ppermute | solution.py:298
  65.8 12.9 %collective-permute-done.25.refs_2_ = bf16[256,1536]{1,0:T(8,128)(2,1)} collective-permute-done((bf16[256,1536]{1,0:T(8,128)(2,1)}, bf16[256,1536]{1,0:T(8,128)(2,1)}, u32[]{:S(2)}, u32[]{:S(2)}) %collective-permute-start.25) | collective-permute-done | bytes 786464 | tf_op jit(solution)/shard_map/ppermute | solution.py:298
  97.8 8.3 %collective-permute-done.31.refs_13_ = bf16[64,1536]{1,0:T(8,128)(2,1)} collective-permute-done((bf16[64,1536]{1,0:T(8,128)(2,1)}, bf16[64,1536]{1,0:T(8,128)(2,1)}, u32[]{:S(2)}, u32[]{:S(2)}) %collective-permute-start.31) | collective-permute-done | bytes 196640 | tf_op jit(solution)/shard_map/ppermute | solution.py:293
  124.3 6.0 collective-permute-done.45.refs_3_
  146.9 9.2 %collective-permute-done.49.refs_13_ = bf16[64,1536]{1,0:T(8,128)(2,1)} collective-permute-done((bf16[64,1536]{1,0:T(8,128)(2,1)}, bf16[64,1536]{1,0:T(8,128)(2,1)}, u32[]{:S(2)}, u32[]{:S(2)}) %collective-permute-start.49) | collective-permute-done | bytes 196640 | tf_op jit(solution)/shard_map/ppermute | solution.py:293
  156.2 5.1 shard_map.63
  185.1 8.2 %collective-permute-done.44.refs_2_ = bf16[256,1536]{1,0:T(8,128)(2,1)} collective-permute-done((bf16[256,1536]{1,0:T(8,128)(2,1)}, bf16[256,1536]{1,0:T(8,128)(2,1)}, u32[]{:S(2)}, u32[]{:S(2)}) %collective-permute-start.44) | collective-permute-done | bytes 786464 | tf_op jit(solution)/shard_map/ppermute | solution.py:298
  195.5 5.1 shard_map.64
  205.1 5.9 collective-permute-done.67.refs_13_
  241.7 6.8 %collective-permute-done.62.refs_2_ = bf16[256,1536]{1,0:T(8,128)(2,1)} collective-permute-done((bf16[256,1536]{1,0:T(8,128)(2,1)}, bf16[256,1536]{1,0:T(8,128)(2,1)}, u32[]{:S(2)}, u32[]{:S(2)}) %collective-permute-start.62) | collective-permute-done | bytes 786464 | tf_op jit(solution)/shard_map/ppermute | solution.py:298
  260.0 5.5 collective-permute-done.85.refs_13_
  267.2 5.2 shard_map.71
  295.0 7.7 %collective-permute-done.80.refs_2_ = bf16[256,1536]{1,0:T(8,128)(2,1)} collective-permute-done((bf16[256,1536]{1,0:T(8,128)(2,1)}, bf16[256,1536]{1,0:T(8,128)(2,1)}, u32[]{:S(2)}, u32[]{:S(2)}) %collective-permute-start.80) | collective-permute-done | bytes 786464 | tf_op jit(solution)/shard_map/ppermute | solution.py:298
  316.3 7.1 %collective-permute-done.103.refs_13_ = bf16[64,1536]{1,0:T(8,128)(2,1)} collective-permute-done((bf16[64,1536]{1,0:T(8,128)(2,1)}, bf16[64,1536]{1,0:T(8,128)(2,1)}, u32[]{:S(2)}, u32[]{:S(2)}) %collective-permute-start.103) | collective-permute-done | bytes 196640 | tf_op jit(solution)/shard_map/ppermute | solution.py:293
  324.9 5.1 shard_map.75
  353.5 7.1 %collective-permute-done.98.refs_2_ = bf16[256,1536]{1,0:T(8,128)(2,1)} collective-permute-done((bf16[256,1536]{1,0:T(8,128)(2,1)}, bf16[256,1536]{1,0:T(8,128)(2,1)}, u32[]{:S(2)}, u32[]{:S(2)}) %collective-permute-start.98) | collective-permute-done | bytes 786464 | tf_op jit(solution)/shard_map/ppermute | solution.py:298
  408.3 6.7 %collective-permute-done.116.refs_2_ = bf16[256,1536]{1,0:T(8,128)(2,1)} collective-permute-done((bf16[256,1536]{1,0:T(8,128)(2,1)}, bf16[256,1536]{1,0:T(8,128)(2,1)}, u32[]{:S(2)}, u32[]{:S(2)}) %collective-permute-start.116) | collective-permute-done | bytes 786464 | tf_op jit(solution)/shard_map/ppermute | solution.py:298
  428.6 6.9 %collective-permute-done.139.refs_13_ = bf16[64,1536]{1,0:T(8,128)(2,1)} collective-permute-done((bf16[64,1536]{1,0:T(8,128)(2,1)}, bf16[64,1536]{1,0:T(8,128)(2,1)}, u32[]{:S(2)}, u32[]{:S(2)}) %collective-permute-start.139) | collective-permute-done | bytes 196640 | tf_op jit(solution)/shard_map/ppermute | solution.py:293
  436.9 5.1 shard_map.83
  465.5 7.1 %collective-permute-done.134.refs_2_ = bf16[256,1536]{1,0:T(8,128)(2,1)} collective-permute-done((bf16[256,1536]{1,0:T(8,128)(2,1)}, bf16[256,1536]{1,0:T(8,128)(2,1)}, u32[]{:S(2)}, u32[]{:S(2)}) %collective-permute-start.134) | collective-permute-done | bytes 786464 | tf_op jit(solution)/shard_map/ppermute | solution.py:298
  475.7 5.1 shard_map.84
  484.4 5.7 collective-permute-done.157.refs_13_
  491.9 5.1 shard_map.87
  513.9 5.1 shard_map.88
  519.0 8.3 %collective-permute-done.152.refs_2_ = bf16[256,1536]{1,0:T(8,128)(2,1)} collective-permute-done((bf16[256,1536]{1,0:T(8,128)(2,1)}, bf16[256,1536]{1,0:T(8,128)(2,1)}, u32[]{:S(2)}, u32[]{:S(2)}) %collective-permute-start.152) | collective-permute-done | bytes 786464 | tf_op jit(solution)/shard_map/ppermute | solution.py:298
  539.0 6.4 collective-permute-done.188.refs_11_
  545.4 5.1 shard_map.91
  586.0 5.1 collective-permute-done.181.refs_10_
  599.9 9.7 %collective-permute-done.173.refs_10_ = bf16[64,1536]{1,0:T(8,128)(2,1)} collective-permute-done((bf16[64,1536]{1,0:T(8,128)(2,1)}, bf16[64,1536]{1,0:T(8,128)(2,1)}, u32[]{:S(2)}, u32[]{:S(2)}) %collective-permute-start.173) | collective-permute-done | bytes 196640 | tf_op jit(solution)/shard_map/ppermute | solution.py:293
  612.4 5.5 collective-permute-done.198.refs_25_
  634.4 9.4 %collective-permute-done.165.refs_10_ = bf16[64,1536]{1,0:T(8,128)(2,1)} collective-permute-done((bf16[64,1536]{1,0:T(8,128)(2,1)}, bf16[64,1536]{1,0:T(8,128)(2,1)}, u32[]{:S(2)}, u32[]{:S(2)}) %collective-permute-start.165) | collective-permute-done | bytes 196640 | tf_op jit(solution)/shard_map/ppermute | solution.py:293
  (437 shorter events, 436.6 us)
Async XLA Ops:
  13.8 33.8 %collective-permute-start.24 = (bf16[256,1536]{1,0:T(8,128)(2,1)}, bf16[256,1536]{1,0:T(8,128)(2,1)}, u32[]{:S(2)}, u32[]{:S(2)}) collective-permute-start(bf16[256,1536]{1,0:T(8,128)(2,1)} %slice.12), channel_id=1, source_target_pairs={{0,8},{8,0},{16,24},{24,16},{1,9},{9,1},{17,25},{25,17},{2,10},{10... | collective-permute-start | bytes 2359304 | tf_op jit(solution)/shard_map/ppermute | solution.py:298
  35.6 28.9 %collective-permute-start.5 = (bf16[256,1536]{1,0:T(8,128)(2,1)}, bf16[256,1536]{1,0:T(8,128)(2,1)}, u32[]{:S(2)}, u32[]{:S(2)}) collective-permute-start(bf16[256,1536]{1,0:T(8,128)(2,1)} %get-tuple-element.157), channel_id=1, source_target_pairs={{0,8},{8,0},{16,24},{24,16},{1,9},{9,1},{17,25},{25,17},{2,10},{10... | collective-permute-start | bytes 2359304 | tf_op jit(solution)/shard_map/ppermute | solution.py:298
  50.8 27.9 %collective-permute-start.25 = (bf16[256,1536]{1,0:T(8,128)(2,1)}, bf16[256,1536]{1,0:T(8,128)(2,1)}, u32[]{:S(2)}, u32[]{:S(2)}) collective-permute-start(bf16[256,1536]{1,0:T(8,128)(2,1)} %get-tuple-element.172), channel_id=1, source_target_pairs={{0,8},{8,0},{16,24},{24,16},{1,9},{9,1},{17,25},{25,17},{2,10},{10... | collective-permute-start | bytes 2359304 | tf_op jit(solution)/shard_map/ppermute | solution.py:298
  52.4 29.6 %collective-permute-start.27 = (bf16[256,1536]{1,0:T(8,128)(2,1)}, bf16[256,1536]{1,0:T(8,128)(2,1)}, u32[]{:S(2)}, u32[]{:S(2)}) collective-permute-start(bf16[256,1536]{1,0:T(8,128)(2,1)} %get-tuple-element.174), channel_id=1, source_target_pairs={{0,16},{8,24},{16,0},{24,8},{1,17},{9,25},{17,1},{25,9},{2,18},{10... | collective-permute-start | bytes 2359304 | tf_op jit(solution)/shard_map/ppermute | solution.py:290
  57.5 29.6 %collective-permute-start.9 = (bf16[64,1536]{1,0:T(8,128)(2,1)}, bf16[64,1536]{1,0:T(8,128)(2,1)}, u32[]{:S(2)}, u32[]{:S(2)}) collective-permute-start(bf16[64,1536]{1,0:T(8,128)(2,1)} %get-tuple-element.161), channel_id=1, source_target_pairs={{0,2},{1,3},{2,0},{3,1},{4,6},{5,7},{6,4},{7,5},{8,10},{9,11},{10,... | collective-permute-start | bytes 589832 | tf_op jit(solution)/shard_map/ppermute | solution.py:293
  59.1 29.6 %collective-permute-start.11 = (bf16[64,1536]{1,0:T(8,128)(2,1)}, bf16[64,1536]{1,0:T(8,128)(2,1)}, u32[]{:S(2)}, u32[]{:S(2)}) collective-permute-start(bf16[64,1536]{1,0:T(8,128)(2,1)} %get-tuple-element.162), channel_id=1, source_target_pairs={{0,4},{1,5},{2,6},{3,7},{4,0},{5,1},{6,2},{7,3},{8,12},{9,13},{10,... | collective-permute-start | bytes 589832 | tf_op jit(solution)/shard_map/ppermute | solution.py:293
  82.0 32.0 %collective-permute-start.16 = (bf16[256,1536]{1,0:T(8,128)(2,1)}, bf16[256,1536]{1,0:T(8,128)(2,1)}, u32[]{:S(2)}, u32[]{:S(2)}) collective-permute-start(bf16[256,1536]{1,0:T(8,128)(2,1)} %get-tuple-element.165), channel_id=1, source_target_pairs={{0,16},{8,24},{16,0},{24,8},{1,17},{9,25},{17,1},{25,9},{2,18},{10... | collective-permute-start | bytes 2359304 | tf_op jit(solution)/shard_map/ppermute | solution.py:290
  96.3 25.6 %collective-permute-start.6 = (bf16[256,1536]{1,0:T(8,128)(2,1)}, bf16[256,1536]{1,0:T(8,128)(2,1)}, u32[]{:S(2)}, u32[]{:S(2)}) collective-permute-start(bf16[256,1536]{1,0:T(8,128)(2,1)} %get-tuple-element.158), channel_id=1, source_target_pairs={{0,8},{8,0},{16,24},{24,16},{1,9},{9,1},{17,25},{25,17},{2,10},{10... | collective-permute-start | bytes 2359304 | tf_op jit(solution)/shard_map/ppermute | solution.py:298
  163.4 29.9 %collective-permute-start.44 = (bf16[256,1536]{1,0:T(8,128)(2,1)}, bf16[256,1536]{1,0:T(8,128)(2,1)}, u32[]{:S(2)}, u32[]{:S(2)}) collective-permute-start(bf16[256,1536]{1,0:T(8,128)(2,1)} %get-tuple-element.187), channel_id=1, source_target_pairs={{0,8},{8,0},{16,24},{24,16},{1,9},{9,1},{17,25},{25,17},{2,10},{10... | collective-permute-start | bytes 2359304 | tf_op jit(solution)/shard_map/ppermute | solution.py:298
  176.9 25.3 %collective-permute-start.42 = (bf16[64,1536]{1,0:T(8,128)(2,1)}, bf16[64,1536]{1,0:T(8,128)(2,1)}, u32[]{:S(2)}, u32[]{:S(2)}) collective-permute-start(bf16[64,1536]{1,0:T(8,128)(2,1)} %get-tuple-element.186), channel_id=1, source_target_pairs={{0,6},{1,7},{2,4},{3,5},{4,2},{5,3},{6,0},{7,1},{8,14},{9,15},{10,... | collective-permute-start | bytes 589832 | tf_op jit(solution)/shard_map/ppermute | solution.py:293
  218.5 29.9 %collective-permute-start.62 = (bf16[256,1536]{1,0:T(8,128)(2,1)}, bf16[256,1536]{1,0:T(8,128)(2,1)}, u32[]{:S(2)}, u32[]{:S(2)}) collective-permute-start(bf16[256,1536]{1,0:T(8,128)(2,1)} %get-tuple-element.201), channel_id=1, source_target_pairs={{0,8},{8,0},{16,24},{24,16},{1,9},{9,1},{17,25},{25,17},{2,10},{10... | collective-permute-start | bytes 2359304 | tf_op jit(solution)/shard_map/ppermute | solution.py:298
  231.0 25.2 %collective-permute-start.58 = (bf16[64,1536]{1,0:T(8,128)(2,1)}, bf16[64,1536]{1,0:T(8,128)(2,1)}, u32[]{:S(2)}, u32[]{:S(2)}) collective-permute-start(bf16[64,1536]{1,0:T(8,128)(2,1)} %get-tuple-element.199), channel_id=1, source_target_pairs={{0,4},{1,5},{2,6},{3,7},{4,0},{5,1},{6,2},{7,3},{8,12},{9,13},{10,... | collective-permute-start | bytes 589832 | tf_op jit(solution)/shard_map/ppermute | solution.py:293
  231.8 25.9 %collective-permute-start.60 = (bf16[64,1536]{1,0:T(8,128)(2,1)}, bf16[64,1536]{1,0:T(8,128)(2,1)}, u32[]{:S(2)}, u32[]{:S(2)}) collective-permute-start(bf16[64,1536]{1,0:T(8,128)(2,1)} %get-tuple-element.200), channel_id=1, source_target_pairs={{0,6},{1,7},{2,4},{3,5},{4,2},{5,3},{6,0},{7,1},{8,14},{9,15},{10,... | collective-permute-start | bytes 589832 | tf_op jit(solution)/shard_map/ppermute | solution.py:293
  273.2 29.4 %collective-permute-start.80 = (bf16[256,1536]{1,0:T(8,128)(2,1)}, bf16[256,1536]{1,0:T(8,128)(2,1)}, u32[]{:S(2)}, u32[]{:S(2)}) collective-permute-start(bf16[256,1536]{1,0:T(8,128)(2,1)} %get-tuple-element.215), channel_id=1, source_target_pairs={{0,8},{8,0},{16,24},{24,16},{1,9},{9,1},{17,25},{25,17},{2,10},{10... | collective-permute-start | bytes 2359304 | tf_op jit(solution)/shard_map/ppermute | solution.py:298
  286.6 25.6 %collective-permute-start.76 = (bf16[64,1536]{1,0:T(8,128)(2,1)}, bf16[64,1536]{1,0:T(8,128)(2,1)}, u32[]{:S(2)}, u32[]{:S(2)}) collective-permute-start(bf16[64,1536]{1,0:T(8,128)(2,1)} %get-tuple-element.213), channel_id=1, source_target_pairs={{0,4},{1,5},{2,6},{3,7},{4,0},{5,1},{6,2},{7,3},{8,12},{9,13},{10,... | collective-permute-start | bytes 589832 | tf_op jit(solution)/shard_map/ppermute | solution.py:293
  287.7 26.0 %collective-permute-start.78 = (bf16[64,1536]{1,0:T(8,128)(2,1)}, bf16[64,1536]{1,0:T(8,128)(2,1)}, u32[]{:S(2)}, u32[]{:S(2)}) collective-permute-start(bf16[64,1536]{1,0:T(8,128)(2,1)} %get-tuple-element.214), channel_id=1, source_target_pairs={{0,6},{1,7},{2,4},{3,5},{4,2},{5,3},{6,0},{7,1},{8,14},{9,15},{10,... | collective-permute-start | bytes 589832 | tf_op jit(solution)/shard_map/ppermute | solution.py:293
  330.4 30.2 %collective-permute-start.98 = (bf16[256,1536]{1,0:T(8,128)(2,1)}, bf16[256,1536]{1,0:T(8,128)(2,1)}, u32[]{:S(2)}, u32[]{:S(2)}) collective-permute-start(bf16[256,1536]{1,0:T(8,128)(2,1)} %get-tuple-element.229), channel_id=1, source_target_pairs={{0,8},{8,0},{16,24},{24,16},{1,9},{9,1},{17,25},{25,17},{2,10},{10... | collective-permute-start | bytes 2359304 | tf_op jit(solution)/shard_map/ppermute | solution.py:298
  343.3 25.4 %collective-permute-start.94 = (bf16[64,1536]{1,0:T(8,128)(2,1)}, bf16[64,1536]{1,0:T(8,128)(2,1)}, u32[]{:S(2)}, u32[]{:S(2)}) collective-permute-start(bf16[64,1536]{1,0:T(8,128)(2,1)} %get-tuple-element.227), channel_id=1, source_target_pairs={{0,4},{1,5},{2,6},{3,7},{4,0},{5,1},{6,2},{7,3},{8,12},{9,13},{10,... | collective-permute-start | bytes 589832 | tf_op jit(solution)/shard_map/ppermute | solution.py:293
  344.2 26.0 %collective-permute-start.96 = (bf16[64,1536]{1,0:T(8,128)(2,1)}, bf16[64,1536]{1,0:T(8,128)(2,1)}, u32[]{:S(2)}, u32[]{:S(2)}) collective-permute-start(bf16[64,1536]{1,0:T(8,128)(2,1)} %get-tuple-element.228), channel_id=1, source_target_pairs={{0,6},{1,7},{2,4},{3,5},{4,2},{5,3},{6,0},{7,1},{8,14},{9,15},{10,... | collective-permute-start | bytes 589832 | tf_op jit(solution)/shard_map/ppermute | solution.py:293
  385.5 29.6 %collective-permute-start.116 = (bf16[256,1536]{1,0:T(8,128)(2,1)}, bf16[256,1536]{1,0:T(8,128)(2,1)}, u32[]{:S(2)}, u32[]{:S(2)}) collective-permute-start(bf16[256,1536]{1,0:T(8,128)(2,1)} %get-tuple-element.243), channel_id=1, source_target_pairs={{0,8},{8,0},{16,24},{24,16},{1,9},{9,1},{17,25},{25,17},{2,10},{10... | collective-permute-start | bytes 2359304 | tf_op jit(solution)/shard_map/ppermute | solution.py:298
  398.9 25.5 %collective-permute-start.112 = (bf16[64,1536]{1,0:T(8,128)(2,1)}, bf16[64,1536]{1,0:T(8,128)(2,1)}, u32[]{:S(2)}, u32[]{:S(2)}) collective-permute-start(bf16[64,1536]{1,0:T(8,128)(2,1)} %get-tuple-element.241), channel_id=1, source_target_pairs={{0,4},{1,5},{2,6},{3,7},{4,0},{5,1},{6,2},{7,3},{8,12},{9,13},{10,... | collective-permute-start | bytes 589832 | tf_op jit(solution)/shard_map/ppermute | solution.py:293
  399.8 25.9 %collective-permute-start.114 = (bf16[64,1536]{1,0:T(8,128)(2,1)}, bf16[64,1536]{1,0:T(8,128)(2,1)}, u32[]{:S(2)}, u32[]{:S(2)}) collective-permute-start(bf16[64,1536]{1,0:T(8,128)(2,1)} %get-tuple-element.242), channel_id=1, source_target_pairs={{0,6},{1,7},{2,4},{3,5},{4,2},{5,3},{6,0},{7,1},{8,14},{9,15},{10,... | collective-permute-start | bytes 589832 | tf_op jit(solution)/shard_map/ppermute | solution.py:293
  442.1 30.4 %collective-permute-start.134 = (bf16[256,1536]{1,0:T(8,128)(2,1)}, bf16[256,1536]{1,0:T(8,128)(2,1)}, u32[]{:S(2)}, u32[]{:S(2)}) collective-permute-start(bf16[256,1536]{1,0:T(8,128)(2,1)} %get-tuple-element.257), channel_id=1, source_target_pairs={{0,8},{8,0},{16,24},{24,16},{1,9},{9,1},{17,25},{25,17},{2,10},{10... | collective-permute-start | bytes 2359304 | tf_op jit(solution)/shard_map/ppermute | solution.py:298
  455.4 25.4 %collective-permute-start.130 = (bf16[64,1536]{1,0:T(8,128)(2,1)}, bf16[64,1536]{1,0:T(8,128)(2,1)}, u32[]{:S(2)}, u32[]{:S(2)}) collective-permute-start(bf16[64,1536]{1,0:T(8,128)(2,1)} %get-tuple-element.255), channel_id=1, source_target_pairs={{0,4},{1,5},{2,6},{3,7},{4,0},{5,1},{6,2},{7,3},{8,12},{9,13},{10,... | collective-permute-start | bytes 589832 | tf_op jit(solution)/shard_map/ppermute | solution.py:293
  456.2 26.0 %collective-permute-start.132 = (bf16[64,1536]{1,0:T(8,128)(2,1)}, bf16[64,1536]{1,0:T(8,128)(2,1)}, u32[]{:S(2)}, u32[]{:S(2)}) collective-permute-start(bf16[64,1536]{1,0:T(8,128)(2,1)} %get-tuple-element.256), channel_id=1, source_target_pairs={{0,6},{1,7},{2,4},{3,5},{4,2},{5,3},{6,0},{7,1},{8,14},{9,15},{10,... | collective-permute-start | bytes 589832 | tf_op jit(solution)/shard_map/ppermute | solution.py:293
  497.0 30.3 %collective-permute-start.152 = (bf16[256,1536]{1,0:T(8,128)(2,1)}, bf16[256,1536]{1,0:T(8,128)(2,1)}, u32[]{:S(2)}, u32[]{:S(2)}) collective-permute-start(bf16[256,1536]{1,0:T(8,128)(2,1)} %get-tuple-element.271), channel_id=1, source_target_pairs={{0,8},{8,0},{16,24},{24,16},{1,9},{9,1},{17,25},{25,17},{2,10},{10... | collective-permute-start | bytes 2359304 | tf_op jit(solution)/shard_map/ppermute | solution.py:298
  497.3 31.8 %collective-permute-start.186 = (bf16[256,1536]{1,0:T(8,128)(2,1)}, bf16[256,1536]{1,0:T(8,128)(2,1)}, u32[]{:S(2)}, u32[]{:S(2)}) collective-permute-start(bf16[256,1536]{1,0:T(8,128)(2,1)} %get-tuple-element.295), channel_id=1, source_target_pairs={{0,16},{8,24},{16,0},{24,8},{1,17},{9,25},{17,1},{25,9},{2,18},{10... | collective-permute-start | bytes 2359304 | tf_op jit(solution)/shard_map/ppermute | solution.py:290
  506.6 25.9 %collective-permute-start.146 = (bf16[64,1536]{1,0:T(8,128)(2,1)}, bf16[64,1536]{1,0:T(8,128)(2,1)}, u32[]{:S(2)}, u32[]{:S(2)}) collective-permute-start(bf16[64,1536]{1,0:T(8,128)(2,1)} %get-tuple-element.268), channel_id=1, source_target_pairs={{0,2},{1,3},{2,0},{3,1},{4,6},{5,7},{6,4},{7,5},{8,10},{9,11},{10,... | collective-permute-start | bytes 589832 | tf_op jit(solution)/shard_map/ppermute | solution.py:293
  511.1 25.3 %collective-permute-start.148 = (bf16[64,1536]{1,0:T(8,128)(2,1)}, bf16[64,1536]{1,0:T(8,128)(2,1)}, u32[]{:S(2)}, u32[]{:S(2)}) collective-permute-start(bf16[64,1536]{1,0:T(8,128)(2,1)} %get-tuple-element.269), channel_id=1, source_target_pairs={{0,4},{1,5},{2,6},{3,7},{4,0},{5,1},{6,2},{7,3},{8,12},{9,13},{10,... | collective-permute-start | bytes 589832 | tf_op jit(solution)/shard_map/ppermute | solution.py:293
  527.3 30.8 %collective-permute-start.143 = (bf16[256,1536]{1,0:T(8,128)(2,1)}, bf16[256,1536]{1,0:T(8,128)(2,1)}, u32[]{:S(2)}, u32[]{:S(2)}) collective-permute-start(bf16[256,1536]{1,0:T(8,128)(2,1)} %get-tuple-element.265), channel_id=1, source_target_pairs={{0,8},{8,0},{16,24},{24,16},{1,9},{9,1},{17,25},{25,17},{2,10},{10... | collective-permute-start | bytes 2359304 | tf_op jit(solution)/shard_map/ppermute | solution.py:298
  536.4 29.8 %collective-permute-start.177 = (bf16[256,1536]{1,0:T(8,128)(2,1)}, bf16[256,1536]{1,0:T(8,128)(2,1)}, u32[]{:S(2)}, u32[]{:S(2)}) collective-permute-start(bf16[256,1536]{1,0:T(8,128)(2,1)} %get-tuple-element.289), channel_id=1, source_target_pairs={{0,16},{8,24},{16,0},{24,8},{1,17},{9,25},{17,1},{25,9},{2,18},{10... | collective-permute-start | bytes 2359304 | tf_op jit(solution)/shard_map/ppermute | solution.py:290
  566.3 52.1 %collective-permute-start.161 = (bf16[256,1536]{1,0:T(8,128)(2,1)}, bf16[256,1536]{1,0:T(8,128)(2,1)}, u32[]{:S(2)}, u32[]{:S(2)}) collective-permute-start(bf16[256,1536]{1,0:T(8,128)(2,1)} %get-tuple-element.279), channel_id=1, source_target_pairs={{0,16},{8,24},{16,0},{24,8},{1,17},{9,25},{17,1},{25,9},{2,18},{10... | collective-permute-start | bytes 2359304 | tf_op jit(solution)/shard_map/ppermute | solution.py:290
  (171 other events, 2209.9 us)

commit v3 on v2

--- a/solution.py
+++ b/solution.py
@@ -9,7 +9,7 @@
 
 UNITS = 3
 TILES = 2
-AHEAD = 2
+AHEAD = 3
 LAG = 4
 VMEM = 67_000_000
 
@@ -28,7 +28,8 @@
 
 def chunks_of(cols, virt):
     step = UNITS * virt
-    return [(start, min(step, cols - start)) for start in range(0, cols, step)]
+    edges = [0, *range(cols % step or step, cols + 1, step)]
+    return [(a, b - a) for a, b in zip(edges, edges[1:])]
 
 
 class Contract:
@@ -149,9 +150,7 @@
 
 class Update:
     def __init__(self, old, other, moved, source, energy, virt_energy, start, out):
-        self.start, self.prev, self.host = start, out, None
-        if isinstance(out, Update):
-            self.prev, self.host = None, out
+        self.start, self.prev = start, out
         rows, columns = old.shape
         self.n_col, self.width = len(moved), moved[0].shape[1]
         self.cols, self.rows, self.virt = columns // self.n_col, rows, virt_energy.shape[0]
@@ -165,7 +164,7 @@
         if self.prev is not None:
             self.ins.append(out)
             self.in_specs.append(pl.BlockSpec(memory_space=pl.ANY))
-        self.out_shape = [] if self.host else [jax.ShapeDtypeStruct((rows, columns), old.dtype)]
+        self.out_shape = [jax.ShapeDtypeStruct((rows, columns), old.dtype)]
         self.scratch = [pltpu.VMEM((self.n_col, rows, self.width), jnp.bfloat16)] * 4 + [
             pltpu.SemaphoreType.DMA((3, self.n_col)),
             pltpu.SemaphoreType.DMA((self.n_col,)),
@@ -176,7 +175,7 @@
     def bind(self, ins, outs, scratch):
         self.source, self.va, self.e, self.vb, self.old, self.other = ins[:6]
         self.moved = ins[6 : 6 + self.n_col]
-        self.out = self.host.out if self.host else outs[0]
+        (self.out,) = outs
         self.old_buf, self.other_buf, self.moved_buf, self.new_buf, self.in_sem, self.out_sem = scratch
 
     def place(self, m):
@@ -328,6 +327,7 @@
         start = chunks[k][0]
         return Update(amps_old, other_terms, moved[k], source, energy, virt_energy, start, onto)
 
+    far[1], energy, source = lax.optimization_barrier((far[1], energy, source))
     for k, (start, width) in enumerate(chunks):
         ahead = chunks[k + AHEAD] if k + AHEAD < count else None
         job = Contract(panel, range(1, n_hi), integrals, far[k], start, ahead=ahead)
@@ -344,10 +344,8 @@
             if m:
                 block = trade(block, 2 * m)
             moved[k] += [block, trade(block, 1)]
-    for k in (count - 4, count - 3):
+    for k in range(count - LAG, count):
         ((out,),) = call(renew(k, out))
-    first = renew(count - 2, out)
-    (out,), _ = call(first, renew(count - 1, first))
     return out
 
 

time: 662 us -> 677 us (1.023)
  waiting for transfers between devices: 263 us -> 272 us
    ppermute x157, waiting for transfers between devices: 139 us -> 219 us  [trade(): return lax.ppermute(value, 'col', [(c, c ^ m) for c in range(n_col)])]
    ppermute x22, waiting for transfers between devices: 94.6 us -> 51.3 us  [fetch(): far[k] = lax.ppermute(piece, 'row', swap)]
    ppermute x23, waiting for transfers between devices: 29.2 us -> 1.95 us  [shift(): return lax.ppermute(value, 'row', perm)]
    pallas_call x47 -> x48, Pallas kernels: 191 us -> 193 us  [call(): pl.pallas_call(functools.partial(kernel, jobs), in_specs=flat('in_specs')...]
  transfers between devices with their start and end apart: 202 -> 202, of which waited for: 61 -> 54; matrix products, arithmetic and copies ran while one was open for 1% -> 1% of each run, Pallas kernels for 28% -> 28%
where the time goes in v3:
time: 677 us; the launch traced here: 673 us
  waiting for transfers between devices  272 us (40%)
  starting transfers between devices  197 us (29%)
  Pallas kernels  193 us (29%)
  local copies, waits for them, and re-layouts  7.5 us (1%)
    ppermute x157, waiting for transfers between devices, trade(): return lax.ppermute(value, 'col', [(c, c ^ m) for c in range(n_col)])  219 us
    pallas_call x48, Pallas kernels, call(): pl.pallas_call(functools.partial(kernel, jobs), in_specs=flat('in_specs')...  193 us
    ppermute x157, starting transfers between devices, trade(): return lax.ppermute(value, 'col', [(c, c ^ m) for c in range(n_col)])  136 us
    ppermute x22, waiting for transfers between devices, fetch(): far[k] = lax.ppermute(piece, 'row', swap)  51.3 us
    ppermute x22, starting transfers between devices, fetch(): far[k] = lax.ppermute(piece, 'row', swap)  30.7 us
    ppermute x23, starting transfers between devices, shift(): return lax.ppermute(value, 'row', perm)  30.4 us
  transfers between devices with their start and end apart: 202, of which 54 were waited for; matrix products, arithmetic and copies ran while one was open for 1% of the time, Pallas kernels for 28%

profile of v3, /device:TPU:0, one launch (start us, length us, event | category | flops | bytes accessed | tf_op | source)
XLA Modules:
  0.0 673.3 jit_solution(6220610995584675818)
XLA Ops:
  28.7 25.8 %collective-permute-done.refs_2_ = bf16[256,1536]{1,0:T(8,128)(2,1)} collective-permute-done((bf16[256,1536]{1,0:T(8,128)(2,1)}, bf16[256,1536]{1,0:T(8,128)(2,1)}, u32[]{:S(2)}, u32[]{:S(2)}) %collective-permute-start) | collective-permute-done | bytes 786464 | tf_op jit(solution)/shard_map/ppermute | solution.py:297
  86.0 16.7 %collective-permute-done.26.refs_2_ = bf16[256,1536]{1,0:T(8,128)(2,1)} collective-permute-done((bf16[256,1536]{1,0:T(8,128)(2,1)}, bf16[256,1536]{1,0:T(8,128)(2,1)}, u32[]{:S(2)}, u32[]{:S(2)}) %collective-permute-start.26) | collective-permute-done | bytes 786464 | tf_op jit(solution)/shard_map/ppermute | solution.py:297
  120.8 5.2 collective-permute-done.11.refs_11_
  151.0 5.3 collective-permute-done.56.refs_11_
  156.3 9.5 %collective-permute-done.58.refs_13_ = bf16[64,1536]{1,0:T(8,128)(2,1)} collective-permute-done((bf16[64,1536]{1,0:T(8,128)(2,1)}, bf16[64,1536]{1,0:T(8,128)(2,1)}, u32[]{:S(2)}, u32[]{:S(2)}) %collective-permute-start.58) | collective-permute-done | bytes 196640 | tf_op jit(solution)/shard_map/ppermute | solution.py:292
  166.2 5.1 shard_map.63
  178.9 5.1 shard_map.64
  192.2 5.9 collective-permute-start.35
  208.8 5.1 shard_map.68
  229.1 11.5 %collective-permute-done.85.refs_13_ = bf16[64,1536]{1,0:T(8,128)(2,1)} collective-permute-done((bf16[64,1536]{1,0:T(8,128)(2,1)}, bf16[64,1536]{1,0:T(8,128)(2,1)}, u32[]{:S(2)}, u32[]{:S(2)}) %collective-permute-start.85) | collective-permute-done | bytes 196640 | tf_op jit(solution)/shard_map/ppermute | solution.py:292
  260.1 5.8 collective-permute-done.74.refs_11_
  265.9 9.2 %collective-permute-done.76.refs_13_ = bf16[64,1536]{1,0:T(8,128)(2,1)} collective-permute-done((bf16[64,1536]{1,0:T(8,128)(2,1)}, bf16[64,1536]{1,0:T(8,128)(2,1)}, u32[]{:S(2)}, u32[]{:S(2)}) %collective-permute-start.76) | collective-permute-done | bytes 196640 | tf_op jit(solution)/shard_map/ppermute | solution.py:292
  275.6 5.2 shard_map.70
  288.5 5.1 shard_map.74
  299.7 6.3 collective-permute-done.67.refs_13_
  318.3 5.1 shard_map.75
  341.6 9.9 %collective-permute-done.103.refs_13_ = bf16[64,1536]{1,0:T(8,128)(2,1)} collective-permute-done((bf16[64,1536]{1,0:T(8,128)(2,1)}, bf16[64,1536]{1,0:T(8,128)(2,1)}, u32[]{:S(2)}, u32[]{:S(2)}) %collective-permute-start.103) | collective-permute-done | bytes 196640 | tf_op jit(solution)/shard_map/ppermute | solution.py:292
  370.6 6.9 %collective-permute-done.92.refs_11_ = bf16[64,1536]{1,0:T(8,128)(2,1)} collective-permute-done((bf16[64,1536]{1,0:T(8,128)(2,1)}, bf16[64,1536]{1,0:T(8,128)(2,1)}, u32[]{:S(2)}, u32[]{:S(2)}) %collective-permute-start.92) | collective-permute-done | bytes 196640 | tf_op jit(solution)/shard_map/ppermute | solution.py:292
  377.6 7.8 %collective-permute-done.94.refs_13_ = bf16[64,1536]{1,0:T(8,128)(2,1)} collective-permute-done((bf16[64,1536]{1,0:T(8,128)(2,1)}, bf16[64,1536]{1,0:T(8,128)(2,1)}, u32[]{:S(2)}, u32[]{:S(2)}) %collective-permute-start.94) | collective-permute-done | bytes 196640 | tf_op jit(solution)/shard_map/ppermute | solution.py:292
  411.9 5.9 collective-permute-done.141.refs_15_
  429.0 5.1 shard_map.82
  450.9 12.1 %collective-permute-done.121.refs_13_ = bf16[64,1536]{1,0:T(8,128)(2,1)} collective-permute-done((bf16[64,1536]{1,0:T(8,128)(2,1)}, bf16[64,1536]{1,0:T(8,128)(2,1)}, u32[]{:S(2)}, u32[]{:S(2)}) %collective-permute-start.121) | collective-permute-done | bytes 196640 | tf_op jit(solution)/shard_map/ppermute | solution.py:292
  482.2 6.2 collective-permute-done.164.refs_11_
  488.4 8.8 %collective-permute-done.166.refs_13_ = bf16[64,1536]{1,0:T(8,128)(2,1)} collective-permute-done((bf16[64,1536]{1,0:T(8,128)(2,1)}, bf16[64,1536]{1,0:T(8,128)(2,1)}, u32[]{:S(2)}, u32[]{:S(2)}) %collective-permute-start.166) | collective-permute-done | bytes 196640 | tf_op jit(solution)/shard_map/ppermute | solution.py:292
  510.8 5.1 shard_map.88
  547.3 5.9 collective-permute-done.146.refs_11_
  553.2 9.0 %collective-permute-done.148.refs_13_ = bf16[64,1536]{1,0:T(8,128)(2,1)} collective-permute-done((bf16[64,1536]{1,0:T(8,128)(2,1)}, bf16[64,1536]{1,0:T(8,128)(2,1)}, u32[]{:S(2)}, u32[]{:S(2)}) %collective-permute-start.148) | collective-permute-done | bytes 196640 | tf_op jit(solution)/shard_map/ppermute | solution.py:292
  585.1 7.4 %collective-permute-done.198.refs_10_ = bf16[64,1536]{1,0:T(8,128)(2,1)} collective-permute-done((bf16[64,1536]{1,0:T(8,128)(2,1)}, bf16[64,1536]{1,0:T(8,128)(2,1)}, u32[]{:S(2)}, u32[]{:S(2)}) %collective-permute-start.198) | collective-permute-done | bytes 196640 | tf_op jit(solution)/shard_map/ppermute | solution.py:292
  602.9 6.2 collective-permute-done.188.refs_8_
  609.1 8.8 %collective-permute-done.190.refs_10_ = bf16[64,1536]{1,0:T(8,128)(2,1)} collective-permute-done((bf16[64,1536]{1,0:T(8,128)(2,1)}, bf16[64,1536]{1,0:T(8,128)(2,1)}, u32[]{:S(2)}, u32[]{:S(2)}) %collective-permute-start.190) | collective-permute-done | bytes 196640 | tf_op jit(solution)/shard_map/ppermute | solution.py:292
  631.9 7.6 %collective-permute-done.182.refs_10_ = bf16[64,1536]{1,0:T(8,128)(2,1)} collective-permute-done((bf16[64,1536]{1,0:T(8,128)(2,1)}, bf16[64,1536]{1,0:T(8,128)(2,1)}, u32[]{:S(2)}, u32[]{:S(2)}) %collective-permute-start.182) | collective-permute-done | bytes 196640 | tf_op jit(solution)/shard_map/ppermute | solution.py:292
  650.1 7.7 %collective-permute-done.174.refs_10_ = bf16[64,1536]{1,0:T(8,128)(2,1)} collective-permute-done((bf16[64,1536]{1,0:T(8,128)(2,1)}, bf16[64,1536]{1,0:T(8,128)(2,1)}, u32[]{:S(2)}, u32[]{:S(2)}) %collective-permute-start.174) | collective-permute-done | bytes 196640 | tf_op jit(solution)/shard_map/ppermute | solution.py:292
  (437 shorter events, 420.1 us)
Async XLA Ops:
  19.9 46.8 %collective-permute-start.8 = (bf16[256,1536]{1,0:T(8,128)(2,1)}, bf16[256,1536]{1,0:T(8,128)(2,1)}, u32[]{:S(2)}, u32[]{:S(2)}) collective-permute-start(bf16[256,1536]{1,0:T(8,128)(2,1)} %slice.16), channel_id=1, source_target_pairs={{0,8},{8,0},{16,24},{24,16},{1,9},{9,1},{17,25},{25,17},{2,10},{10... | collective-permute-start | bytes 2359304 | tf_op jit(solution)/shard_map/ppermute | solution.py:297
  20.4 34.0 %collective-permute-start = (bf16[256,1536]{1,0:T(8,128)(2,1)}, bf16[256,1536]{1,0:T(8,128)(2,1)}, u32[]{:S(2)}, u32[]{:S(2)}) collective-permute-start(bf16[256,1536]{1,0:T(8,128)(2,1)} %slice.14), channel_id=1, source_target_pairs={{0,8},{8,0},{16,24},{24,16},{1,9},{9,1},{17,25},{25,17},{2,10},{10... | collective-permute-start | bytes 2359304 | tf_op jit(solution)/shard_map/ppermute | solution.py:297
  27.1 32.2 %collective-permute-start.27 = (bf16[256,512]{1,0:T(8,128)(2,1)}, bf16[256,512]{1,0:T(8,128)(2,1)}, u32[]{:S(2)}, u32[]{:S(2)}) collective-permute-start(bf16[256,512]{1,0:T(8,128)(2,1)} %get-tuple-element.182), channel_id=1, source_target_pairs={{0,16},{8,24},{16,0},{24,8},{1,17},{9,25},{17,1},{25,9},{2,18},{10... | collective-permute-start | bytes 786440 | tf_op jit(solution)/shard_map/ppermute | solution.py:289
  73.2 29.6 %collective-permute-start.26 = (bf16[256,1536]{1,0:T(8,128)(2,1)}, bf16[256,1536]{1,0:T(8,128)(2,1)}, u32[]{:S(2)}, u32[]{:S(2)}) collective-permute-start(bf16[256,1536]{1,0:T(8,128)(2,1)} %get-tuple-element.181), channel_id=1, source_target_pairs={{0,8},{8,0},{16,24},{24,16},{1,9},{9,1},{17,25},{25,17},{2,10},{10... | collective-permute-start | bytes 2359304 | tf_op jit(solution)/shard_map/ppermute | solution.py:297
  73.7 30.5 %collective-permute-start.9 = (bf16[256,1536]{1,0:T(8,128)(2,1)}, bf16[256,1536]{1,0:T(8,128)(2,1)}, u32[]{:S(2)}, u32[]{:S(2)}) collective-permute-start(bf16[256,1536]{1,0:T(8,128)(2,1)} %get-tuple-element.169), channel_id=1, source_target_pairs={{0,16},{8,24},{16,0},{24,8},{1,17},{9,25},{17,1},{25,9},{2,18},{10... | collective-permute-start | bytes 2359304 | tf_op jit(solution)/shard_map/ppermute | solution.py:289
  75.8 40.0 %collective-permute-start.17 = (bf16[256,1536]{1,0:T(8,128)(2,1)}, bf16[256,1536]{1,0:T(8,128)(2,1)}, u32[]{:S(2)}, u32[]{:S(2)}) collective-permute-start(bf16[256,1536]{1,0:T(8,128)(2,1)} %get-tuple-element.174), channel_id=1, source_target_pairs={{0,8},{8,0},{16,24},{24,16},{1,9},{9,1},{17,25},{25,17},{2,10},{10... | collective-permute-start | bytes 2359304 | tf_op jit(solution)/shard_map/ppermute | solution.py:297
  80.8 35.6 %collective-permute-start.20 = (bf16[64,1536]{1,0:T(8,128)(2,1)}, bf16[64,1536]{1,0:T(8,128)(2,1)}, u32[]{:S(2)}, u32[]{:S(2)}) collective-permute-start(bf16[64,1536]{1,0:T(8,128)(2,1)} %get-tuple-element.178), channel_id=1, source_target_pairs={{0,2},{1,3},{2,0},{3,1},{4,6},{5,7},{6,4},{7,5},{8,10},{9,11},{10,... | collective-permute-start | bytes 589832 | tf_op jit(solution)/shard_map/ppermute | solution.py:292
  85.9 32.1 %collective-permute-start.22 = (bf16[64,1536]{1,0:T(8,128)(2,1)}, bf16[64,1536]{1,0:T(8,128)(2,1)}, u32[]{:S(2)}, u32[]{:S(2)}) collective-permute-start(bf16[64,1536]{1,0:T(8,128)(2,1)} %get-tuple-element.179), channel_id=1, source_target_pairs={{0,4},{1,5},{2,6},{3,7},{4,0},{5,1},{6,2},{7,3},{8,12},{9,13},{10,... | collective-permute-start | bytes 589832 | tf_op jit(solution)/shard_map/ppermute | solution.py:292
  139.3 32.6 %collective-permute-start.45 = (bf16[256,1536]{1,0:T(8,128)(2,1)}, bf16[256,1536]{1,0:T(8,128)(2,1)}, u32[]{:S(2)}, u32[]{:S(2)}) collective-permute-start(bf16[256,1536]{1,0:T(8,128)(2,1)} %get-tuple-element.196), channel_id=1, source_target_pairs={{0,16},{8,24},{16,0},{24,8},{1,17},{9,25},{17,1},{25,9},{2,18},{10... | collective-permute-start | bytes 2359304 | tf_op jit(solution)/shard_map/ppermute | solution.py:289
  140.9 31.1 %collective-permute-start.53 = (bf16[256,1536]{1,0:T(8,128)(2,1)}, bf16[256,1536]{1,0:T(8,128)(2,1)}, u32[]{:S(2)}, u32[]{:S(2)}) collective-permute-start(bf16[256,1536]{1,0:T(8,128)(2,1)} %get-tuple-element.201), channel_id=1, source_target_pairs={{0,8},{8,0},{16,24},{24,16},{1,9},{9,1},{17,25},{25,17},{2,10},{10... | collective-permute-start | bytes 2359304 | tf_op jit(solution)/shard_map/ppermute | solution.py:297
  171.3 28.7 %collective-permute-start.36 = (bf16[256,1536]{1,0:T(8,128)(2,1)}, bf16[256,1536]{1,0:T(8,128)(2,1)}, u32[]{:S(2)}, u32[]{:S(2)}) collective-permute-start(bf16[256,1536]{1,0:T(8,128)(2,1)} %get-tuple-element.190), channel_id=1, source_target_pairs={{0,16},{8,24},{16,0},{24,8},{1,17},{9,25},{17,1},{25,9},{2,18},{10... | collective-permute-start | bytes 2359304 | tf_op jit(solution)/shard_map/ppermute | solution.py:289
  171.9 28.5 %collective-permute-start.44 = (bf16[256,1536]{1,0:T(8,128)(2,1)}, bf16[256,1536]{1,0:T(8,128)(2,1)}, u32[]{:S(2)}, u32[]{:S(2)}) collective-permute-start(bf16[256,1536]{1,0:T(8,128)(2,1)} %get-tuple-element.195), channel_id=1, source_target_pairs={{0,8},{8,0},{16,24},{24,16},{1,9},{9,1},{17,25},{25,17},{2,10},{10... | collective-permute-start | bytes 2359304 | tf_op jit(solution)/shard_map/ppermute | solution.py:297
  217.3 33.7 %collective-permute-start.72 = (bf16[256,1536]{1,0:T(8,128)(2,1)}, bf16[256,1536]{1,0:T(8,128)(2,1)}, u32[]{:S(2)}, u32[]{:S(2)}) collective-permute-start(bf16[256,1536]{1,0:T(8,128)(2,1)} %get-tuple-element.217), channel_id=1, source_target_pairs={{0,16},{8,24},{16,0},{24,8},{1,17},{9,25},{17,1},{25,9},{2,18},{10... | collective-permute-start | bytes 2359304 | tf_op jit(solution)/shard_map/ppermute | solution.py:289
  227.5 30.2 %collective-permute-start.80 = (bf16[256,1536]{1,0:T(8,128)(2,1)}, bf16[256,1536]{1,0:T(8,128)(2,1)}, u32[]{:S(2)}, u32[]{:S(2)}) collective-permute-start(bf16[256,1536]{1,0:T(8,128)(2,1)} %get-tuple-element.222), channel_id=1, source_target_pairs={{0,8},{8,0},{16,24},{24,16},{1,9},{9,1},{17,25},{25,17},{2,10},{10... | collective-permute-start | bytes 2359304 | tf_op jit(solution)/shard_map/ppermute | solution.py:297
  247.6 33.5 %collective-permute-start.63 = (bf16[256,1536]{1,0:T(8,128)(2,1)}, bf16[256,1536]{1,0:T(8,128)(2,1)}, u32[]{:S(2)}, u32[]{:S(2)}) collective-permute-start(bf16[256,1536]{1,0:T(8,128)(2,1)} %get-tuple-element.211), channel_id=1, source_target_pairs={{0,16},{8,24},{16,0},{24,8},{1,17},{9,25},{17,1},{25,9},{2,18},{10... | collective-permute-start | bytes 2359304 | tf_op jit(solution)/shard_map/ppermute | solution.py:289
  249.2 32.5 %collective-permute-start.71 = (bf16[256,1536]{1,0:T(8,128)(2,1)}, bf16[256,1536]{1,0:T(8,128)(2,1)}, u32[]{:S(2)}, u32[]{:S(2)}) collective-permute-start(bf16[256,1536]{1,0:T(8,128)(2,1)} %get-tuple-element.216), channel_id=1, source_target_pairs={{0,8},{8,0},{16,24},{24,16},{1,9},{9,1},{17,25},{25,17},{2,10},{10... | collective-permute-start | bytes 2359304 | tf_op jit(solution)/shard_map/ppermute | solution.py:297
  323.4 37.1 %collective-permute-start.90 = (bf16[256,1536]{1,0:T(8,128)(2,1)}, bf16[256,1536]{1,0:T(8,128)(2,1)}, u32[]{:S(2)}, u32[]{:S(2)}) collective-permute-start(bf16[256,1536]{1,0:T(8,128)(2,1)} %get-tuple-element.232), channel_id=1, source_target_pairs={{0,16},{8,24},{16,0},{24,8},{1,17},{9,25},{17,1},{25,9},{2,18},{10... | collective-permute-start | bytes 2359304 | tf_op jit(solution)/shard_map/ppermute | solution.py:289
  324.9 36.1 %collective-permute-start.98 = (bf16[256,1536]{1,0:T(8,128)(2,1)}, bf16[256,1536]{1,0:T(8,128)(2,1)}, u32[]{:S(2)}, u32[]{:S(2)}) collective-permute-start(bf16[256,1536]{1,0:T(8,128)(2,1)} %get-tuple-element.237), channel_id=1, source_target_pairs={{0,8},{8,0},{16,24},{24,16},{1,9},{9,1},{17,25},{25,17},{2,10},{10... | collective-permute-start | bytes 2359304 | tf_op jit(solution)/shard_map/ppermute | solution.py:297
  357.2 34.4 %collective-permute-start.89 = (bf16[256,1536]{1,0:T(8,128)(2,1)}, bf16[256,1536]{1,0:T(8,128)(2,1)}, u32[]{:S(2)}, u32[]{:S(2)}) collective-permute-start(bf16[256,1536]{1,0:T(8,128)(2,1)} %get-tuple-element.231), channel_id=1, source_target_pairs={{0,8},{8,0},{16,24},{24,16},{1,9},{9,1},{17,25},{25,17},{2,10},{10... | collective-permute-start | bytes 2359304 | tf_op jit(solution)/shard_map/ppermute | solution.py:297
  359.0 32.9 %collective-permute-start.135 = (bf16[256,1536]{1,0:T(8,128)(2,1)}, bf16[256,1536]{1,0:T(8,128)(2,1)}, u32[]{:S(2)}, u32[]{:S(2)}) collective-permute-start(bf16[256,1536]{1,0:T(8,128)(2,1)} %get-tuple-element.265), channel_id=1, source_target_pairs={{0,16},{8,24},{16,0},{24,8},{1,17},{9,25},{17,1},{25,9},{2,18},{10... | collective-permute-start | bytes 2359304 | tf_op jit(solution)/shard_map/ppermute | solution.py:289
  391.0 28.8 %collective-permute-start.126 = (bf16[256,1536]{1,0:T(8,128)(2,1)}, bf16[256,1536]{1,0:T(8,128)(2,1)}, u32[]{:S(2)}, u32[]{:S(2)}) collective-permute-start(bf16[256,1536]{1,0:T(8,128)(2,1)} %get-tuple-element.259), channel_id=1, source_target_pairs={{0,16},{8,24},{16,0},{24,8},{1,17},{9,25},{17,1},{25,9},{2,18},{10... | collective-permute-start | bytes 2359304 | tf_op jit(solution)/shard_map/ppermute | solution.py:289
  391.6 28.6 %collective-permute-start.134 = (bf16[256,1536]{1,0:T(8,128)(2,1)}, bf16[256,1536]{1,0:T(8,128)(2,1)}, u32[]{:S(2)}, u32[]{:S(2)}) collective-permute-start(bf16[256,1536]{1,0:T(8,128)(2,1)} %get-tuple-element.264), channel_id=1, source_target_pairs={{0,8},{8,0},{16,24},{24,16},{1,9},{9,1},{17,25},{25,17},{2,10},{10... | collective-permute-start | bytes 2359304 | tf_op jit(solution)/shard_map/ppermute | solution.py:297
  434.1 38.1 %collective-permute-start.116 = (bf16[256,1536]{1,0:T(8,128)(2,1)}, bf16[256,1536]{1,0:T(8,128)(2,1)}, u32[]{:S(2)}, u32[]{:S(2)}) collective-permute-start(bf16[256,1536]{1,0:T(8,128)(2,1)} %get-tuple-element.252), channel_id=1, source_target_pairs={{0,8},{8,0},{16,24},{24,16},{1,9},{9,1},{17,25},{25,17},{2,10},{10... | collective-permute-start | bytes 2359304 | tf_op jit(solution)/shard_map/ppermute | solution.py:297
  436.0 36.7 %collective-permute-start.162 = (bf16[256,1536]{1,0:T(8,128)(2,1)}, bf16[256,1536]{1,0:T(8,128)(2,1)}, u32[]{:S(2)}, u32[]{:S(2)}) collective-permute-start(bf16[256,1536]{1,0:T(8,128)(2,1)} %get-tuple-element.286), channel_id=1, source_target_pairs={{0,16},{8,24},{16,0},{24,8},{1,17},{9,25},{17,1},{25,9},{2,18},{10... | collective-permute-start | bytes 2359304 | tf_op jit(solution)/shard_map/ppermute | solution.py:289
  468.7 34.8 %collective-permute-start.153 = (bf16[256,1536]{1,0:T(8,128)(2,1)}, bf16[256,1536]{1,0:T(8,128)(2,1)}, u32[]{:S(2)}, u32[]{:S(2)}) collective-permute-start(bf16[256,1536]{1,0:T(8,128)(2,1)} %get-tuple-element.280), channel_id=1, source_target_pairs={{0,16},{8,24},{16,0},{24,8},{1,17},{9,25},{17,1},{25,9},{2,18},{10... | collective-permute-start | bytes 2359304 | tf_op jit(solution)/shard_map/ppermute | solution.py:289
  470.3 33.3 %collective-permute-start.161 = (bf16[256,1536]{1,0:T(8,128)(2,1)}, bf16[256,1536]{1,0:T(8,128)(2,1)}, u32[]{:S(2)}, u32[]{:S(2)}) collective-permute-start(bf16[256,1536]{1,0:T(8,128)(2,1)} %get-tuple-element.285), channel_id=1, source_target_pairs={{0,8},{8,0},{16,24},{24,16},{1,9},{9,1},{17,25},{25,17},{2,10},{10... | collective-permute-start | bytes 2359304 | tf_op jit(solution)/shard_map/ppermute | solution.py:297
  502.8 27.5 %collective-permute-start.144 = (bf16[256,1536]{1,0:T(8,128)(2,1)}, bf16[256,1536]{1,0:T(8,128)(2,1)}, u32[]{:S(2)}, u32[]{:S(2)}) collective-permute-start(bf16[256,1536]{1,0:T(8,128)(2,1)} %get-tuple-element.274), channel_id=1, source_target_pairs={{0,16},{8,24},{16,0},{24,8},{1,17},{9,25},{17,1},{25,9},{2,18},{10... | collective-permute-start | bytes 2359304 | tf_op jit(solution)/shard_map/ppermute | solution.py:289
  503.4 27.3 %collective-permute-start.152 = (bf16[256,1536]{1,0:T(8,128)(2,1)}, bf16[256,1536]{1,0:T(8,128)(2,1)}, u32[]{:S(2)}, u32[]{:S(2)}) collective-permute-start(bf16[256,1536]{1,0:T(8,128)(2,1)} %get-tuple-element.279), channel_id=1, source_target_pairs={{0,8},{8,0},{16,24},{24,16},{1,9},{9,1},{17,25},{25,17},{2,10},{10... | collective-permute-start | bytes 2359304 | tf_op jit(solution)/shard_map/ppermute | solution.py:297
  515.9 29.0 %collective-permute-start.143 = (bf16[256,1536]{1,0:T(8,128)(2,1)}, bf16[256,1536]{1,0:T(8,128)(2,1)}, u32[]{:S(2)}, u32[]{:S(2)}) collective-permute-start(bf16[256,1536]{1,0:T(8,128)(2,1)} %get-tuple-element.273), channel_id=1, source_target_pairs={{0,8},{8,0},{16,24},{24,16},{1,9},{9,1},{17,25},{25,17},{2,10},{10... | collective-permute-start | bytes 2359304 | tf_op jit(solution)/shard_map/ppermute | solution.py:297
  535.9 57.1 %collective-permute-start.186 = (bf16[256,1536]{1,0:T(8,128)(2,1)}, bf16[256,1536]{1,0:T(8,128)(2,1)}, u32[]{:S(2)}, u32[]{:S(2)}) collective-permute-start(bf16[256,1536]{1,0:T(8,128)(2,1)} %get-tuple-element.304), channel_id=1, source_target_pairs={{0,16},{8,24},{16,0},{24,8},{1,17},{9,25},{17,1},{25,9},{2,18},{10... | collective-permute-start | bytes 2359304 | tf_op jit(solution)/shard_map/ppermute | solution.py:289
  571.3 46.6 %collective-permute-start.178 = (bf16[256,1536]{1,0:T(8,128)(2,1)}, bf16[256,1536]{1,0:T(8,128)(2,1)}, u32[]{:S(2)}, u32[]{:S(2)}) collective-permute-start(bf16[256,1536]{1,0:T(8,128)(2,1)} %get-tuple-element.299), channel_id=1, source_target_pairs={{0,16},{8,24},{16,0},{24,8},{1,17},{9,25},{17,1},{25,9},{2,18},{10... | collective-permute-start | bytes 2359304 | tf_op jit(solution)/shard_map/ppermute | solution.py:289
  583.6 42.9 %collective-permute-start.170 = (bf16[256,1536]{1,0:T(8,128)(2,1)}, bf16[256,1536]{1,0:T(8,128)(2,1)}, u32[]{:S(2)}, u32[]{:S(2)}) collective-permute-start(bf16[256,1536]{1,0:T(8,128)(2,1)} %get-tuple-element.294), channel_id=1, source_target_pairs={{0,16},{8,24},{16,0},{24,8},{1,17},{9,25},{17,1},{25,9},{2,18},{10... | collective-permute-start | bytes 2359304 | tf_op jit(solution)/shard_map/ppermute | solution.py:289
  (170 other events, 2072.3 us)
